TPU v7x, 128 devices: a whole 4x4x4 slice. The times are simulated.
128 devices in a mesh: rows: 16 (over y, z_lo, core), cols: 8 (over x, z_hi).
Axes of the slice: x: 4, y: 4, z: 4 (z_hi: 2, z_lo: 2; z = z_hi * 2 + z_lo), core: 2. Of those that a mesh axis runs over, the one named last changes fastest.
Arguments:
- features: bfloat16 [512, 1024, 192], P('rows', 'cols'), may hold values from -6 to 6
- gain_conv: float32 [192], replicated, may hold values from 0.1 to 1.9
- w_expand: bfloat16 [192, 768], replicated, may hold values from -0.4375 to 0.4375
- w_depth: bfloat16 [3, 3, 768], replicated, may hold values from -2 to 2
- w_project: bfloat16 [768, 192], replicated, may hold values from -0.21875 to 0.21875
- gain_block: float32 [192], replicated, may hold values from 0.1 to 1.9
- qkv_block: bfloat16 [192, 576], replicated, may hold values from -18 to 18, as said below
- out_block: bfloat16 [192, 192], replicated, may hold values from -0.4375 to 0.4375
- gain_bffn: float32 [192], replicated, may hold values from 0.1 to 1.9
- ffn_in_block: bfloat16 [192, 768], replicated, may hold values from -0.4375 to 0.4375
- ffn_out_block: bfloat16 [768, 192], replicated, may hold values from -0.21875 to 0.21875
- gain_grid: float32 [192], replicated, may hold values from 0.1 to 1.9
- qkv_grid: bfloat16 [192, 576], replicated, may hold values from -18 to 18, as said below
- out_grid: bfloat16 [192, 192], replicated, may hold values from -0.4375 to 0.4375
- gain_gffn: float32 [192], replicated, may hold values from 0.1 to 1.9
- ffn_in_grid: bfloat16 [192, 768], replicated, may hold values from -0.4375 to 0.4375
- ffn_out_grid: bfloat16 [768, 192], replicated, may hold values from -0.21875 to 0.21875
Outputs:
- result: bfloat16 [512, 1024, 192], P('rows', 'cols')
Inputs may be any that keep to these rules, and one draw needn't show every extreme that they name: `qkv_block`: columns hold the queries, keys and values, each grouped by head. `qkv_grid`: columns hold the queries, keys and values, each grouped by head.
All inputs are finite; a program needn't handle non-finite values.
Results may differ from a plain program's by a relative error of at most 0.023.
Values may be sent and summed in bfloat16 or wider, within the bound.
A program may use at most 128 MiB of HBM per device.

v0:
```python
import jax
import jax.numpy as jnp
import numpy as np
from jax import lax
from jax.sharding import PartitionSpec as P

HEADS = 6
BLOCK = 8
G = 16


EPSILON = 1e-05


def layer_norm(values, scale_gain):
    values = values.astype(jnp.float32)
    average = jnp.mean(values, axis=-1, keepdims=True)
    centred = values - average
    variance = jnp.mean(centred * centred, axis=-1, keepdims=True)
    return (centred * lax.rsqrt(variance + EPSILON) * scale_gain).astype(jnp.bfloat16)


def gelu_exact(values):
    sqrt_half = np.sqrt(0.5).astype(values.dtype)
    return 0.5 * values * (1.0 + lax.erf(values * sqrt_half))


def project(normed, weight):
    flattened = normed.reshape(-1, normed.shape[-1])
    output = jnp.dot(flattened, weight, preferred_element_type=jnp.float32)
    return output.reshape(normed.shape[:-1] + (weight.shape[1],))


def attend(normed, w_qkv, w_out):
    groups, tokens, channels = normed.shape
    head_size = channels // HEADS
    qkv_all = project(normed, w_qkv).astype(jnp.bfloat16)
    heads_split = qkv_all.reshape(groups, tokens, 3, HEADS, head_size)
    scores = jnp.einsum(
        "gthd,gshd->ghts",
        heads_split[:, :, 0],
        heads_split[:, :, 1],
        preferred_element_type=jnp.float32,
    ) * head_size ** (-0.5)
    weights = jax.nn.softmax(scores, axis=-1).astype(jnp.bfloat16)
    mixed = jnp.einsum(
        "ghts,gshd->gthd", weights, heads_split[:, :, 2], preferred_element_type=jnp.float32
    )
    mixed = mixed.astype(jnp.bfloat16).reshape(groups, tokens, channels)
    return project(mixed, w_out)


def feed_forward(resid, scale_gain, w_in, w_out):
    normed = layer_norm(resid, scale_gain)
    inner_act = gelu_exact(project(normed, w_in)).astype(jnp.bfloat16)
    return (resid.astype(jnp.float32) + project(inner_act, w_out)).astype(jnp.bfloat16)


def shards_body(
    features,
    gain_conv,
    w_expand,
    w_depth,
    w_project,
    gain_block,
    qkv_block,
    out_block,
    gain_bffn,
    ffn_in_block,
    ffn_out_block,
    gain_grid,
    qkv_grid,
    out_grid,
    gain_gffn,
    ffn_in_grid,
    ffn_out_grid,
):
    rows_count = lax.axis_size("rows")
    cols_count = lax.axis_size("cols")
    tile_rows, tile_cols, channels = features.shape
    hidden_width = w_expand.shape[1]

    def expand(cells):
        return gelu_exact(project(layer_norm(cells, gain_conv), w_expand)).astype(jnp.bfloat16)

    both = ("rows", "cols")
    row_forward = [(i, i + 1) for i in range(rows_count - 1)]
    row_backward = [(t, s) for s, t in row_forward]
    col_forward = [(i, i + 1) for i in range(cols_count - 1)]
    col_backward = [(t, s) for s, t in col_forward]
    last_r, last_c = tile_rows - 1, tile_cols - 1
    top_row = lax.ppermute(features[last_r], "rows", row_forward)
    bottom_row = lax.ppermute(features[0], "rows", row_backward)
    left_source = jnp.concatenate(
        [top_row[last_c:], features[:, last_c], bottom_row[last_c:]], axis=0
    )
    right_source = jnp.concatenate([top_row[:1], features[:, 0], bottom_row[:1]], axis=0)
    left_col = lax.ppermute(left_source, "cols", col_forward)
    right_col = lax.ppermute(right_source, "cols", col_backward)
    interior_normed = layer_norm(features, gain_conv)
    interior = gelu_exact(project(interior_normed, w_expand)).astype(jnp.bfloat16)
    halo_cells = jnp.concatenate([top_row, bottom_row, left_col, right_col], axis=0)
    halo = expand(halo_cells)
    top = halo[:tile_cols][None]
    bottom = halo[tile_cols : 2 * tile_cols][None]
    left = halo[2 * tile_cols : 2 * tile_cols + tile_rows + 2][:, None]
    right = halo[2 * tile_cols + tile_rows + 2 :][:, None]
    expanded = jnp.concatenate([top, interior, bottom], axis=0)
    expanded = jnp.concatenate([left, expanded, right], axis=1)
    summed = jnp.zeros((tile_rows, tile_cols, hidden_width), jnp.float32)
    for row_tap in range(3):
        for col_tap in range(3):
            summed = summed + expanded[
                row_tap : row_tap + tile_rows, col_tap : col_tap + tile_cols
            ].astype(jnp.float32) * w_depth[row_tap, col_tap].astype(jnp.float32)
    depthwise = gelu_exact(summed).astype(jnp.bfloat16)
    conv_out = (features.astype(jnp.float32) + project(depthwise, w_project)).astype(jnp.bfloat16)
    win_rows = tile_rows // BLOCK
    win_cols = tile_cols // BLOCK
    windows = (
        conv_out.reshape(win_rows, BLOCK, win_cols, BLOCK, channels)
        .transpose(0, 2, 1, 3, 4)
        .reshape(win_rows * win_cols, BLOCK * BLOCK, channels)
    )
    windows = lax.optimization_barrier(windows)
    update = attend(layer_norm(windows, gain_block), qkv_block, out_block)
    mixed_after = (windows.astype(jnp.float32) + update).astype(jnp.bfloat16)
    mixed_after = feed_forward(mixed_after, gain_bffn, ffn_in_block, ffn_out_block)
    block_out = (
        mixed_after.reshape(win_rows, win_cols, BLOCK, BLOCK, channels)
        .transpose(0, 2, 1, 3, 4)
        .reshape(tile_rows, tile_cols, channels)
    )
    local_rows = G // rows_count
    local_cols = G // cols_count
    stride_rows = tile_rows // local_rows
    stride_cols = tile_cols // local_cols
    part_rows = stride_rows // rows_count
    part_cols = stride_cols // cols_count
    devices = rows_count * cols_count
    split = block_out.reshape(
        local_rows, rows_count, part_rows, local_cols, cols_count, part_cols, channels
    ).transpose(1, 4, 2, 5, 0, 3, 6)
    piece = (part_rows, part_cols, local_rows * local_cols, channels)
    packed = split.reshape(devices, -1, 128)
    received = lax.all_to_all(packed, both, split_axis=0, concat_axis=0, tiled=True)
    tokens = (
        received.reshape((devices,) + piece)
        .transpose(1, 2, 0, 3, 4)
        .reshape(part_rows * part_cols, G * G, channels)
    )
    tokens = lax.optimization_barrier(tokens)
    update = attend(layer_norm(tokens, gain_grid), qkv_grid, out_grid).astype(jnp.bfloat16)
    grid_attn = (tokens.astype(jnp.float32) + update.astype(jnp.float32)).astype(jnp.bfloat16)
    grid_out = feed_forward(grid_attn, gain_gffn, ffn_in_grid, ffn_out_grid)
    grid_out = grid_out.reshape(part_rows, part_cols, devices, local_rows * local_cols, channels)
    packed = grid_out.transpose(2, 0, 1, 3, 4).reshape(devices, -1, 128)
    returned = lax.all_to_all(packed, both, split_axis=0, concat_axis=0, tiled=True)
    return (
        returned.reshape(
            rows_count, cols_count, part_rows, part_cols, local_rows, local_cols, channels
        )
        .transpose(4, 0, 2, 5, 1, 3, 6)
        .reshape(tile_rows, tile_cols, channels)
    )


def solution(mesh):
    return jax.shard_map(
        shards_body,
        mesh=mesh,
        in_specs=(
            P("rows", "cols", None),
            P(),
            P(),
            P(),
            P(),
            P(),
            P(),
            P(),
            P(),
            P(),
            P(),
            P(),
            P(),
            P(),
            P(),
            P(),
            P(),
        ),
        out_specs=P("rows", "cols", None),
        check_vma=False,
    )
```

profile of v0, /device:TPU:1, one launch (start us, length us, event | category | flops | bytes accessed | tf_op | source)
XLA Modules:
  0.0 270.5 jit_solution(341777258583930123)
XLA Ops:
  0.0 0.9 fusion.119
  0.9 0.7 copy.95
  1.6 3.3 %collective-permute-start.1 = (bf16[128,192]{1,0:T(8,128)(2,1)}, bf16[128,192]{1,0:T(8,128)(2,1)S(1)}, u32[]{:S(2)}, u32[]{:S(2)}) collective-permute-start(bf16[128,192]{1,0:T(8,128)(2,1)} %bitcast.1), channel_id=1, source_target_pairs={{8,0},{16,8},{24,16},{32,24},{40,32},{48,40},{56,48},{64,56},{72,6... | collective-permute-start | bytes 147464 | tf_op jit(solution)/shard_map/ppermute | solution.py:93
  5.6 3.5 %collective-permute-start = (bf16[128,192]{1,0:T(8,128)(2,1)}, bf16[128,192]{1,0:T(8,128)(2,1)}, u32[]{:S(2)}, u32[]{:S(2)}) collective-permute-start(bf16[128,192]{1,0:T(8,128)(2,1)} %bitcast), channel_id=1, source_target_pairs={{0,8},{8,16},{16,24},{24,32},{32,40},{40,48},{48,56},{56,64},{64,7... | collective-permute-start | bytes 147464 | tf_op jit(solution)/shard_map/ppermute | solution.py:92
  9.2 1.7 convert_reduce_fusion.4
  10.9 1.9 fusion.43
  12.8 5.9 %multiply_convert_fusion.3 = bf16[32,128,768]{2,1,0:T(8,128)(2,1)} fusion(bf16[32,128,192]{1,2,0:T(8,128)(2,1)} %param.17, f32[192]{0:T(256)} %param.18, f32[32,128]{1,0:T(8,128)S(1)} %add_rsqrt_fusion.4, f32[32,128]{1,0:T(8,128)S(1)} %broadcast_multiply_fusion.4, bf16[192,768]{1,0:T(8,128)(2,1)S(1)} %copy-done), kind=kOutput, calls=%fused_computation.12 | convolution fusion | flops 1227620352 | bytes 8192768 | tf_op jit(solution)/shard_map/dot_general | solution.py:30
  18.7 1.8 fusion.118
  20.5 1.9 copy.96
  22.4 0.9 copy.97
  24.0 1.3 collective-permute-start.3
  25.4 6.4 %collective-permute-start.2 = (bf16[34,192]{1,0:T(8,128)(2,1)S(1)}, bf16[34,192]{1,0:T(8,128)(2,1)S(1)}, u32[]{:S(2)}, u32[]{:S(2)}) collective-permute-start(bf16[34,192]{1,0:T(8,128)(2,1)S(1)} %pad_maximum_fusion.4), channel_id=1, source_target_pairs={{0,1},{1,2},{2,3},{3,4},{4,5},{5,6},{6,7},{8,9},{9,10},{10,11},{11... | collective-permute-start | bytes 39176 | tf_op jit(solution)/shard_map/ppermute | solution.py:98
  31.7 0.9 convert_reduce_fusion.14
  32.7 1.0 convert_reduce_fusion.5
  33.7 1.1 fusion.87
  34.8 1.2 multiply_convert_fusion.13
  36.3 10.1 %maximum_maximum_fusion = (bf16[34,129,768]{2,1,0:T(8,128)(2,1)S(1)}, bf16[34,129,768]{2,1,0:T(8,128)(2,1)S(1)}) fusion(bf16[1,128,768]{2,1,0:T(8,128)(2,1)S(1)} %get-tuple-element.23, bf16[32,128,768]{2,1,0:T(8,128)(2,1)} %multiply_convert_fusion.3, bf16[1,128,768]{2,1,0:T(8,128)(2,1)S(1)} %get-tuple-element.22, bf16[34,1,768]{2,1,0:T(2,128)(2,1)S(1)} %copy.64, ...), kind=kLoop, calls=%fused_computation.16 | loop fusion | flops 53895168 | bytes 20262912 | tf_op jit(solution)/shard_map/concatenate | solution.py:109
  46.4 22.0 %fusion.46 = bf16[32,128,192]{1,2,0:T(8,128)(2,1)S(1)} fusion(bf16[32,128,192]{1,2,0:T(8,128)(2,1)S(1)} %copy-done.2, bf16[32,128,768]{2,1,0:T(8,128)(2,1)} %multiply_convert_fusion.3, bf16[34,129,768]{2,1,0:T(8,128)(2,1)S(1)} %get-tuple-element.15, bf16[1,128,768]{2,1,0:T(8,128)(2,1)S(1)} %get-tuple-element.23, ...), kind=kOutput, calls=%fused_computation.69 | convolution fusion | flops 1326710784 | bytes 47910912 | tf_op jit(solution)/shard_map/dot_general | solution.py:30
  68.4 2.6 copy.66
  71.0 1.9 copy.67
  73.6 1.3 fusion.22
  75.0 4.1 %convolution_convert_fusion = bf16[64,64,576]{2,1,0:T(8,128)(2,1)} fusion(bf16[64,64,192]{2,1,0:T(8,128)(2,1)S(1)} %bitcast.131, f32[192]{0:T(256)S(1)} %copy-done.12, f32[64,64]{1,0:T(8,128)S(1)} %add_rsqrt_fusion.1, f32[64,64]{1,0:T(8,128)S(1)} %broadcast_multiply_fusion.1, bf16[192,576]{1,0:T(8,128)(2,1)S(1)} %copy-done.9), kind=kOutput, calls=%fused_computation.76 | convolution fusion | flops 912261120 | bytes 6546176 | tf_op jit(solution)/shard_map/dot_general | solution.py:30
  79.1 10.2 %copy.68 = bf16[64,64,576]{1,2,0:T(8,128)(2,1)} copy(bf16[64,64,576]{2,1,0:T(8,128)(2,1)} %convolution_convert_fusion) | data formatting | bytes 9437184 | tf_op jit(solution)/shard_map/convert_element_type | solution.py:37
  89.3 9.2 %fusion.49 = f32[64,6,64,64]{2,3,1,0:T(8,128)} fusion(bf16[64,64,3,6,32]{1,4,3,2,0:T(8,128)(2,1)} %bitcast.133), kind=kOutput, calls=%fused_computation.73 | convolution fusion | flops 100663296 | bytes 12582912 | tf_op jit(solution)/shard_map/gthd,gshd->ghts/dot_general | solution.py:39
  98.5 16.4 %fusion.122 = (f32[64,6,64]{2,1,0:T(8,128)S(1)}, f32[64,6,64,64]{2,3,1,0:T(8,128)}) fusion(f32[64,6,64,64]{2,3,1,0:T(8,128)} %fusion.49), kind=kOutput, calls=%fused_computation.166 | output fusion | flops 6291519 | bytes 12681216 | tf_op jit(solution)/shard_map/sub | solution.py:45
  114.9 7.3 %fusion.50 = bf16[64,6,32,64]{3,2,1,0:T(8,128)(2,1)S(1)} fusion(f32[64,6,64,64]{2,3,1,0:T(8,128)} %get-tuple-element.29, f32[64,6,64]{2,1,0:T(8,128)S(1)} %get-tuple-element.28, bf16[64,64,3,6,32]{1,4,3,2,0:T(8,128)(2,1)} %bitcast.134), kind=kOutput, calls=%fused_computation.78 | convolution fusion | flops 104595456 | bytes 17399808 | tf_op jit(solution)/shard_map/ghts,gshd->gthd/dot_general | solution.py:46
  122.3 1.6 convert_reduce_fusion
  123.9 1.3 copy-done.3
  125.3 1.3 fusion.19
  126.7 6.3 %fusion.26 = bf16[64,64,192]{2,1,0:T(8,128)(2,1)S(1)} fusion(bf16[64,64,192]{2,1,0:T(8,128)(2,1)} %copy-done.3, f32[192]{0:T(256)S(1)} %copy-done.13, f32[64,64]{1,0:T(8,128)S(1)} %add_rsqrt_fusion, f32[64,64]{1,0:T(8,128)S(1)} %broadcast_multiply_fusion, bf16[768,192]{0,1:T(8,128)(2,1)S(1)} %copy-done.7, bf16[192,768]{1,0:T(8,128)(2,1)S(1)} %copy-done.8), kind=kOutput, calls=%fused_computation.51 | convolution fusion | flops 2437939200 | bytes 3769088 | tf_op jit(solution)/shard_map/dot_general | solution.py:30
  133.2 3.3 %copy.75 = bf16[16,8,2,8,1,2,192]{6,5,3,2,1,0,4:T(2,128)(2,1)S(1)} copy(bf16[16,8,2,8,1,2,192]{6,3,1,5,2,0,4:T(8,128)(2,1)S(1)} %bitcast.140) | data formatting | bytes 3145728 | tf_op jit(solution)/shard_map/transpose | solution.py:143
  136.5 3.0 %reshape.160 = bf16[128,48,128]{2,1,0:T(8,128)(2,1)} reshape(bf16[16,8,2,8,1,2,192]{6,5,3,2,1,0,4:T(2,128)(2,1)S(1)} %copy.75) | data formatting | bytes 3145728 | tf_op jit(solution)/shard_map/reshape | solution.py:145
  139.5 36.9 %all_to_all.10 = bf16[128,48,128]{2,1,0:T(8,128)(2,1)S(1)} all-to-all(bf16[128,48,128]{2,1,0:T(8,128)(2,1)} %reshape.160), channel_id=1, replica_groups=mesh['rows'=16,'cols'=8] {'rows','cols'}, dimensions={0} | all-to-all | bytes 3145728 | tf_op jit(solution)/shard_map/all_to_all | solution.py:146
  176.4 1.1 copy.76
  177.5 3.0 %copy.77 = bf16[2,8,128,2,192]{4,1,0,3,2:T(8,128)(2,1)} copy(bf16[2,8,128,2,192]{2,4,3,1,0:T(8,128)(2,1)S(1)} %bitcast.141) | data formatting | bytes 3145728 | tf_op jit(solution)/shard_map/transpose | solution.py:149
  180.6 3.5 %copy.78 = bf16[16,256,192]{1,2,0:T(8,128)(2,1)S(1)} copy(bf16[16,256,192]{2,0,1:T(8,128)(2,1)} %bitcast.135) | data formatting | bytes 3145728 | tf_op jit(solution)/shard_map/optimization_barrier | solution.py:152
  184.8 3.7 %convolution_convert_fusion.1 = bf16[16,256,576]{1,2,0:T(8,128)(2,1)} fusion(bf16[16,256,192]{1,2,0:T(8,128)(2,1)S(1)} %copy.78, f32[192]{0:T(256)S(1)} %copy-done.14, f32[16,256]{1,0:T(8,128)S(1)} %add_rsqrt_fusion.3, f32[16,256]{1,0:T(8,128)S(1)} %broadcast_multiply_fusion.3, bf16[192,576]{1,0:T(8,128)(2,1)S(1)} %copy-done.10), kind=kOutput, calls=%fused_computation.77 | convolution fusion | flops 912261120 | bytes 6546176 | tf_op jit(solution)/shard_map/dot_general | solution.py:30
  188.5 14.5 %fusion.123 = (f32[16,6,256]{2,1,0:T(8,128)S(1)}, f32[16,6,256,256]{2,3,1,0:T(8,128)}) fusion(bf16[16,256,3,6,32]{1,4,3,2,0:T(8,128)(2,1)} %bitcast.148), kind=kOutput, calls=%fused_computation.167 | convolution fusion | flops 421527808 | bytes 28409856 | tf_op jit(solution)/shard_map/sub | solution.py:45
  203.0 10.9 %fusion.67 = bf16[16,6,32,256]{3,2,1,0:T(8,128)(2,1)S(1)} fusion(f32[16,6,256,256]{2,3,1,0:T(8,128)} %get-tuple-element.33, f32[16,6,256]{2,1,0:T(8,128)S(1)} %get-tuple-element.32, bf16[16,256,3,6,32]{1,4,3,2,0:T(8,128)(2,1)} %bitcast.149), kind=kOutput, calls=%fused_computation.87 | convolution fusion | flops 416022528 | bytes 28409856 | tf_op jit(solution)/shard_map/ghts,gshd->gthd/dot_general | solution.py:46
  214.0 0.8 convert_reduce_fusion.2
  215.2 7.0 %fusion.48 = bf16[16,256,192]{1,2,0:T(8,128)(2,1)} fusion(bf16[16,256,192]{1,2,0:T(8,128)(2,1)S(1)} %get-tuple-element.35, f32[192]{0:T(256)S(1)} %copy-done.15, f32[16,256]{1,0:T(8,128)S(1)} %add_rsqrt_fusion.2, f32[16,256]{1,0:T(8,128)S(1)} %broadcast_multiply_fusion.2, bf16[768,192]{0,1:T(8,128)(2,1)} %param.33, bf16[192,768]{1,0:T(8,128)(2,1)} %param.32), kind=kOutput, calls=%fused_computation.71 | convolution fusion | flops 2437939200 | bytes 3769088 | tf_op jit(solution)/shard_map/dot_general | solution.py:30
  222.2 3.2 %copy.84 = bf16[16,256,192]{2,0,1:T(8,128)(2,1)S(1)} copy(bf16[16,256,192]{1,2,0:T(8,128)(2,1)} %fusion.48) | data formatting | bytes 3145728 | tf_op jit(solution)/shard_map/convert_element_type | solution.py:56
  225.5 2.9 %copy.85 = bf16[128,2,8,2,192]{0,4,3,2,1:T(8,128)(2,1)} copy(bf16[128,2,8,2,192]{4,2,1,3,0:T(8,128)(2,1)S(1)} %bitcast.136) | data formatting | bytes 3145728 | tf_op jit(solution)/shard_map/transpose | solution.py:157
  228.4 2.0 copy.86
  230.4 29.0 %all_to_all.11 = bf16[128,48,128]{2,1,0:T(8,128)(2,1)} all-to-all(bf16[128,48,128]{2,1,0:T(8,128)(2,1)S(1)} %copy.86), channel_id=1, replica_groups=mesh['rows'=16,'cols'=8] {'rows','cols'}, dimensions={0} | all-to-all | bytes 3145728 | tf_op jit(solution)/shard_map/all_to_all | solution.py:158
  259.4 5.1 %reshape.166 = bf16[16,8,2,8,1,2,192]{6,5,3,2,1,0,4:T(2,128)(2,1)S(1)} reshape(bf16[128,48,128]{2,1,0:T(8,128)(2,1)} %all_to_all.11) | data formatting | bytes 3145728 | tf_op jit(solution)/shard_map/reshape | solution.py:160
  264.6 1.8 copy.87
  266.3 3.9 %copy.88 = bf16[32,128,192]{1,2,0:T(8,128)(2,1)} copy(bf16[32,128,192]{2,1,0:T(8,128)(2,1)} %bitcast.139) | data formatting | bytes 3145728 | tf_op jit(solution)/shard_map/reshape | solution.py:164
  (61 shorter events, 3.8 us)
Async XLA Ops:
  0.0 12.8 %copy-start = (bf16[192,768]{1,0:T(8,128)(2,1)S(1)}, bf16[192,768]{1,0:T(8,128)(2,1)}, u32[]{:S(2)}) copy-start(bf16[192,768]{1,0:T(8,128)(2,1)} %param.19) | copy-start | bytes 884740
  1.6 21.7 %collective-permute-start.1 = (bf16[128,192]{1,0:T(8,128)(2,1)}, bf16[128,192]{1,0:T(8,128)(2,1)S(1)}, u32[]{:S(2)}, u32[]{:S(2)}) collective-permute-start(bf16[128,192]{1,0:T(8,128)(2,1)} %bitcast.1), channel_id=1, source_target_pairs={{8,0},{16,8},{24,16},{32,24},{40,32},{48,40},{56,48},{64,56},{72,6... | collective-permute-start | bytes 147464 | tf_op jit(solution)/shard_map/ppermute | solution.py:93
  5.6 17.7 %collective-permute-start = (bf16[128,192]{1,0:T(8,128)(2,1)}, bf16[128,192]{1,0:T(8,128)(2,1)}, u32[]{:S(2)}, u32[]{:S(2)}) collective-permute-start(bf16[128,192]{1,0:T(8,128)(2,1)} %bitcast), channel_id=1, source_target_pairs={{0,8},{8,16},{16,24},{24,32},{32,40},{40,48},{48,56},{56,64},{64,7... | collective-permute-start | bytes 147464 | tf_op jit(solution)/shard_map/ppermute | solution.py:92
  12.8 5.9 %copy-start.2 = (bf16[32,128,192]{1,2,0:T(8,128)(2,1)S(1)}, bf16[32,128,192]{1,2,0:T(8,128)(2,1)}, u32[]{:S(2)}) copy-start(bf16[32,128,192]{1,2,0:T(8,128)(2,1)} %param.17) | copy-start | bytes 4718596
  18.7 16.0 %copy-start.11 = (f32[192]{0:T(256)S(1)}, f32[192]{0:T(256)}, u32[]{:S(2)}) copy-start(f32[192]{0:T(256)} %param.18) | copy-start | bytes 2308
  24.0 8.6 %collective-permute-start.3 = (bf16[34,192]{1,0:T(8,128)(2,1)S(1)}, bf16[34,192]{1,0:T(8,128)(2,1)S(1)}, u32[]{:S(2)}, u32[]{:S(2)}) collective-permute-start(bf16[34,192]{1,0:T(8,128)(2,1)S(1)} %pad_maximum_fusion.5), channel_id=1, source_target_pairs={{1,0},{2,1},{3,2},{4,3},{5,4},{6,5},{7,6},{9,8},{10,9},{11,10},{12... | collective-permute-start | bytes 39176 | tf_op jit(solution)/shard_map/ppermute | solution.py:99
  25.4 7.3 %collective-permute-start.2 = (bf16[34,192]{1,0:T(8,128)(2,1)S(1)}, bf16[34,192]{1,0:T(8,128)(2,1)S(1)}, u32[]{:S(2)}, u32[]{:S(2)}) collective-permute-start(bf16[34,192]{1,0:T(8,128)(2,1)S(1)} %pad_maximum_fusion.4), channel_id=1, source_target_pairs={{0,1},{1,2},{2,3},{3,4},{4,5},{5,6},{6,7},{8,9},{9,10},{10,11},{11... | collective-permute-start | bytes 39176 | tf_op jit(solution)/shard_map/ppermute | solution.py:98
  36.3 10.1 %copy-start.6 = (bf16[768,192]{0,1:T(8,128)(2,1)S(1)}, bf16[768,192]{0,1:T(8,128)(2,1)}, u32[]{:S(2)}) copy-start(bf16[768,192]{0,1:T(8,128)(2,1)} %param.21) | copy-start | bytes 884740
  71.0 3.9 %copy-start.9 = (bf16[192,576]{1,0:T(8,128)(2,1)S(1)}, bf16[192,576]{1,0:T(8,128)(2,1)}, u32[]{:S(2)}) copy-start(bf16[192,576]{1,0:T(8,128)(2,1)} %param.23) | copy-start | bytes 663556
  71.0 3.9 %copy-start.12 = (f32[192]{0:T(256)S(1)}, f32[192]{0:T(256)}, u32[]{:S(2)}) copy-start(f32[192]{0:T(256)} %param.22) | copy-start | bytes 2308
  114.9 7.3 %copy-start.4 = (bf16[192,192]{1,0:T(8,128)(2,1)S(1)}, bf16[192,192]{1,0:T(8,128)(2,1)}, u32[]{:S(2)}) copy-start(bf16[192,192]{1,0:T(8,128)(2,1)} %param.24) | copy-start | bytes 221188
  122.3 4.4 %copy-start.7 = (bf16[768,192]{0,1:T(8,128)(2,1)S(1)}, bf16[768,192]{0,1:T(8,128)(2,1)}, u32[]{:S(2)}) copy-start(bf16[768,192]{0,1:T(8,128)(2,1)} %param.27) | copy-start | bytes 884740
  122.3 4.4 %copy-start.8 = (bf16[192,768]{1,0:T(8,128)(2,1)S(1)}, bf16[192,768]{1,0:T(8,128)(2,1)}, u32[]{:S(2)}) copy-start(bf16[192,768]{1,0:T(8,128)(2,1)} %param.26) | copy-start | bytes 884740
  122.3 4.4 %copy-start.13 = (f32[192]{0:T(256)S(1)}, f32[192]{0:T(256)}, u32[]{:S(2)}) copy-start(f32[192]{0:T(256)} %param.25) | copy-start | bytes 2308
  123.9 1.4 copy-start.3
  177.5 7.2 %copy-start.10 = (bf16[192,576]{1,0:T(8,128)(2,1)S(1)}, bf16[192,576]{1,0:T(8,128)(2,1)}, u32[]{:S(2)}) copy-start(bf16[192,576]{1,0:T(8,128)(2,1)} %param.29) | copy-start | bytes 663556
  177.5 7.2 %copy-start.14 = (f32[192]{0:T(256)S(1)}, f32[192]{0:T(256)}, u32[]{:S(2)}) copy-start(f32[192]{0:T(256)} %param.28) | copy-start | bytes 2308
  203.0 11.0 %copy-start.5 = (bf16[192,192]{1,0:T(8,128)(2,1)S(1)}, bf16[192,192]{1,0:T(8,128)(2,1)}, u32[]{:S(2)}) copy-start(bf16[192,192]{1,0:T(8,128)(2,1)} %param.30) | copy-start | bytes 221188
  213.9 1.3 copy-start.15
  259.4 10.8 %copy-start.1 = (bf16[192,768]{1,0:T(8,128)(2,1)S(1)}, bf16[192,768]{1,0:T(8,128)(2,1)}, u32[]{:S(2)}) copy-start(bf16[192,768]{1,0:T(8,128)(2,1)} %param.19) | copy-start | bytes 884740
where the time goes:
time: 275 us; the launch traced here: 270 us
  matrix products  94.7 us (34%)
  blocking collectives  65.8 us (24%)
  local copies, waits for them, and re-layouts  57.2 us (21%)
  other arithmetic  37.6 us (14%)
  starting transfers between devices  14.5 us (5%)
    all_to_all x2, blocking collectives, shards_body(): lax.all_to_all(packed, both, split_axis=0, concat_axis=0, tiled=True)  65.8 us
    dot_general x9, matrix products, project(): output = jnp.dot(flattened, weight, preferred_element_type=jnp.float32)  52.7 us
    dot_general x2, matrix products, attend(): jnp.einsum('ghts,gshd->gthd', weights, heads_split[:, :, 2], preferred_el...  18.3 us
    sub x1, other arithmetic, attend(): weights = jax.nn.softmax(scores, axis=-1).astype(jnp.bfloat16)  16.4 us
    sub x1, matrix products, attend(): weights = jax.nn.softmax(scores, axis=-1).astype(jnp.bfloat16)  14.5 us
    convert_element_type x1, local copies, waits for them, and re-layouts, attend(): qkv_all = project(normed, w_qkv).astype(jnp.bfloat16)  10.2 us
    concatenate x1, other arithmetic, shards_body(): expanded = jnp.concatenate([left, expanded, right], axis=1)  10.1 us
    dot_general x1, matrix products, attend(): jnp.einsum('gthd,gshd->ghts', heads_split[:, :, 0], heads_split[:, :, 1],...  9.21 us
  transfers between devices with their start and end apart: 4, of which 0 were waited for; matrix products, arithmetic and copies ran while one was open for 6% of the time, Pallas kernels for 0%

commit v1 on v0

--- a/solution.py
+++ b/solution.py
@@ -42,7 +42,10 @@
         heads_split[:, :, 1],
         preferred_element_type=jnp.float32,
     ) * head_size ** (-0.5)
-    weights = jax.nn.softmax(scores, axis=-1).astype(jnp.bfloat16)
+    peak = jnp.max(scores, axis=-1, keepdims=True)
+    lifted = jnp.exp(scores - peak)
+    total = jnp.sum(lifted, axis=-1, keepdims=True)
+    weights = (lifted * (1.0 / total)).astype(jnp.bfloat16)
     mixed = jnp.einsum(
         "ghts,gshd->gthd", weights, heads_split[:, :, 2], preferred_element_type=jnp.float32
     )

time: 275 us -> 275 us (level)
  no operation moved by 1% of the time
where the time goes in v1:
time: 275 us; the launch traced here: 271 us
  matrix products  94.6 us (34%)
  blocking collectives  65.8 us (24%)
  local copies, waits for them, and re-layouts  57.2 us (21%)
  other arithmetic  37.6 us (14%)
  starting transfers between devices  14.5 us (5%)
    all_to_all x2, blocking collectives, shards_body(): lax.all_to_all(packed, both, split_axis=0, concat_axis=0, tiled=True)  65.8 us
    dot_general x9, matrix products, project(): output = jnp.dot(flattened, weight, preferred_element_type=jnp.float32)  52.7 us
    dot_general x2, matrix products, attend(): jnp.einsum('ghts,gshd->gthd', weights, heads_split[:, :, 2], preferred_el...  18.2 us
    sub x1, other arithmetic, attend(): lifted = jnp.exp(scores - peak)  16.4 us
    sub x1, matrix products, attend(): lifted = jnp.exp(scores - peak)  14.5 us
    convert_element_type x1, local copies, waits for them, and re-layouts, attend(): qkv_all = project(normed, w_qkv).astype(jnp.bfloat16)  10.2 us
    concatenate x1, other arithmetic, shards_body(): expanded = jnp.concatenate([left, expanded, right], axis=1)  10.1 us
    dot_general x1, matrix products, attend(): jnp.einsum('gthd,gshd->ghts', heads_split[:, :, 0], heads_split[:, :, 1],...  9.21 us
  transfers between devices with their start and end apart: 4, of which 0 were waited for; matrix products, arithmetic and copies ran while one was open for 6% of the time, Pallas kernels for 0%

profile of v1, /device:TPU:1, one launch (start us, length us, event | category | flops | bytes accessed | tf_op | source)
XLA Modules:
  0.0 270.5 jit_solution(17274077290534935002)
XLA Ops:
  0.0 0.9 fusion.121
  0.9 0.7 copy.95
  1.6 3.3 %collective-permute-start.1 = (bf16[128,192]{1,0:T(8,128)(2,1)}, bf16[128,192]{1,0:T(8,128)(2,1)S(1)}, u32[]{:S(2)}, u32[]{:S(2)}) collective-permute-start(bf16[128,192]{1,0:T(8,128)(2,1)} %bitcast.1), channel_id=1, source_target_pairs={{8,0},{16,8},{24,16},{32,24},{40,32},{48,40},{56,48},{64,56},{72,6... | collective-permute-start | bytes 147464 | tf_op jit(solution)/shard_map/ppermute | solution.py:96
  5.6 3.5 %collective-permute-start = (bf16[128,192]{1,0:T(8,128)(2,1)}, bf16[128,192]{1,0:T(8,128)(2,1)}, u32[]{:S(2)}, u32[]{:S(2)}) collective-permute-start(bf16[128,192]{1,0:T(8,128)(2,1)} %bitcast), channel_id=1, source_target_pairs={{0,8},{8,16},{16,24},{24,32},{32,40},{40,48},{48,56},{56,64},{64,7... | collective-permute-start | bytes 147464 | tf_op jit(solution)/shard_map/ppermute | solution.py:95
  9.2 1.7 convert_reduce_fusion.4
  10.9 1.9 fusion.45
  12.8 5.9 %multiply_convert_fusion.6 = bf16[32,128,768]{2,1,0:T(8,128)(2,1)} fusion(bf16[32,128,192]{1,2,0:T(8,128)(2,1)} %param.17, f32[192]{0:T(256)} %param.18, f32[32,128]{1,0:T(8,128)S(1)} %add_rsqrt_fusion.4, f32[32,128]{1,0:T(8,128)S(1)} %broadcast_multiply_fusion.4, bf16[192,768]{1,0:T(8,128)(2,1)S(1)} %copy-done), kind=kOutput, calls=%fused_computation.14 | convolution fusion | flops 1227620352 | bytes 8192768 | tf_op jit(solution)/shard_map/dot_general | solution.py:30
  18.7 1.8 fusion.120
  20.5 1.9 copy.96
  22.4 0.9 copy.97
  24.0 1.3 collective-permute-start.3
  25.4 6.4 %collective-permute-start.2 = (bf16[34,192]{1,0:T(8,128)(2,1)S(1)}, bf16[34,192]{1,0:T(8,128)(2,1)S(1)}, u32[]{:S(2)}, u32[]{:S(2)}) collective-permute-start(bf16[34,192]{1,0:T(8,128)(2,1)S(1)} %pad_maximum_fusion.4), channel_id=1, source_target_pairs={{0,1},{1,2},{2,3},{3,4},{4,5},{5,6},{6,7},{8,9},{9,10},{10,11},{11... | collective-permute-start | bytes 39176 | tf_op jit(solution)/shard_map/ppermute | solution.py:101
  31.7 0.9 convert_reduce_fusion.14
  32.7 1.0 convert_reduce_fusion.5
  33.7 1.1 fusion.89
  34.8 1.2 multiply_convert_fusion.21
  36.3 10.1 %maximum_maximum_fusion = (bf16[34,129,768]{2,1,0:T(8,128)(2,1)S(1)}, bf16[34,129,768]{2,1,0:T(8,128)(2,1)S(1)}) fusion(bf16[1,128,768]{2,1,0:T(8,128)(2,1)S(1)} %get-tuple-element.23, bf16[32,128,768]{2,1,0:T(8,128)(2,1)} %multiply_convert_fusion.6, bf16[1,128,768]{2,1,0:T(8,128)(2,1)S(1)} %get-tuple-element.22, bf16[34,1,768]{2,1,0:T(2,128)(2,1)S(1)} %copy.64, ...), kind=kLoop, calls=%fused_computation.17 | loop fusion | flops 53895168 | bytes 20262912 | tf_op jit(solution)/shard_map/concatenate | solution.py:112
  46.4 22.0 %fusion.48 = bf16[32,128,192]{1,2,0:T(8,128)(2,1)S(1)} fusion(bf16[32,128,192]{1,2,0:T(8,128)(2,1)S(1)} %copy-done.2, bf16[32,128,768]{2,1,0:T(8,128)(2,1)} %multiply_convert_fusion.6, bf16[34,129,768]{2,1,0:T(8,128)(2,1)S(1)} %get-tuple-element.15, bf16[1,128,768]{2,1,0:T(8,128)(2,1)S(1)} %get-tuple-element.23, ...), kind=kOutput, calls=%fused_computation.71 | convolution fusion | flops 1326710784 | bytes 47910912 | tf_op jit(solution)/shard_map/dot_general | solution.py:30
  68.4 2.6 copy.66
  71.0 1.9 copy.67
  73.6 1.3 fusion.24
  75.0 4.1 %convolution_convert_fusion = bf16[64,64,576]{2,1,0:T(8,128)(2,1)} fusion(bf16[64,64,192]{2,1,0:T(8,128)(2,1)S(1)} %bitcast.133, f32[192]{0:T(256)S(1)} %copy-done.12, f32[64,64]{1,0:T(8,128)S(1)} %add_rsqrt_fusion.1, f32[64,64]{1,0:T(8,128)S(1)} %broadcast_multiply_fusion.1, bf16[192,576]{1,0:T(8,128)(2,1)S(1)} %copy-done.9), kind=kOutput, calls=%fused_computation.78 | convolution fusion | flops 912261120 | bytes 6546176 | tf_op jit(solution)/shard_map/dot_general | solution.py:30
  79.1 10.2 %copy.68 = bf16[64,64,576]{1,2,0:T(8,128)(2,1)} copy(bf16[64,64,576]{2,1,0:T(8,128)(2,1)} %convolution_convert_fusion) | data formatting | bytes 9437184 | tf_op jit(solution)/shard_map/convert_element_type | solution.py:37
  89.3 9.2 %fusion.51 = f32[64,6,64,64]{2,3,1,0:T(8,128)} fusion(bf16[64,64,3,6,32]{1,4,3,2,0:T(8,128)(2,1)} %bitcast.129), kind=kOutput, calls=%fused_computation.75 | convolution fusion | flops 100663296 | bytes 12582912 | tf_op jit(solution)/shard_map/gthd,gshd->ghts/dot_general | solution.py:39
  98.5 16.4 %fusion.124 = (f32[64,6,64]{2,1,0:T(8,128)S(1)}, f32[64,6,64,64]{2,3,1,0:T(8,128)}) fusion(f32[64,6,64,64]{2,3,1,0:T(8,128)} %fusion.51), kind=kOutput, calls=%fused_computation.170 | output fusion | flops 6291519 | bytes 12681216 | tf_op jit(solution)/shard_map/sub | solution.py:46
  115.0 7.3 %fusion.52 = bf16[64,6,32,64]{3,2,1,0:T(8,128)(2,1)S(1)} fusion(f32[64,6,64,64]{2,3,1,0:T(8,128)} %get-tuple-element.29, f32[64,6,64]{2,1,0:T(8,128)S(1)} %broadcast_divide_fusion, bf16[64,64,3,6,32]{1,4,3,2,0:T(8,128)(2,1)} %bitcast.130), kind=kOutput, calls=%fused_computation.80 | convolution fusion | flops 104595456 | bytes 17399808 | tf_op jit(solution)/shard_map/ghts,gshd->gthd/dot_general | solution.py:49
  122.4 1.6 convert_reduce_fusion
  124.0 1.3 copy-done.3
  125.3 1.3 fusion.21
  126.7 6.3 %fusion.28 = bf16[64,64,192]{2,1,0:T(8,128)(2,1)S(1)} fusion(bf16[64,64,192]{2,1,0:T(8,128)(2,1)} %copy-done.3, f32[192]{0:T(256)S(1)} %copy-done.13, f32[64,64]{1,0:T(8,128)S(1)} %add_rsqrt_fusion, f32[64,64]{1,0:T(8,128)S(1)} %broadcast_multiply_fusion, bf16[768,192]{0,1:T(8,128)(2,1)S(1)} %copy-done.7, bf16[192,768]{1,0:T(8,128)(2,1)S(1)} %copy-done.8), kind=kOutput, calls=%fused_computation.53 | convolution fusion | flops 2437939200 | bytes 3769088 | tf_op jit(solution)/shard_map/dot_general | solution.py:30
  133.3 3.3 %copy.75 = bf16[16,8,2,8,1,2,192]{6,5,3,2,1,0,4:T(2,128)(2,1)S(1)} copy(bf16[16,8,2,8,1,2,192]{6,3,1,5,2,0,4:T(8,128)(2,1)S(1)} %bitcast.141) | data formatting | bytes 3145728 | tf_op jit(solution)/shard_map/transpose | solution.py:146
  136.6 3.0 %reshape.166 = bf16[128,48,128]{2,1,0:T(8,128)(2,1)} reshape(bf16[16,8,2,8,1,2,192]{6,5,3,2,1,0,4:T(2,128)(2,1)S(1)} %copy.75) | data formatting | bytes 3145728 | tf_op jit(solution)/shard_map/reshape | solution.py:148
  139.6 36.9 %all_to_all.10 = bf16[128,48,128]{2,1,0:T(8,128)(2,1)S(1)} all-to-all(bf16[128,48,128]{2,1,0:T(8,128)(2,1)} %reshape.166), channel_id=1, replica_groups=mesh['rows'=16,'cols'=8] {'rows','cols'}, dimensions={0} | all-to-all | bytes 3145728 | tf_op jit(solution)/shard_map/all_to_all | solution.py:149
  176.4 1.1 copy.76
  177.6 3.0 %copy.77 = bf16[2,8,128,2,192]{4,1,0,3,2:T(8,128)(2,1)} copy(bf16[2,8,128,2,192]{2,4,3,1,0:T(8,128)(2,1)S(1)} %bitcast.143) | data formatting | bytes 3145728 | tf_op jit(solution)/shard_map/transpose | solution.py:152
  180.6 3.5 %copy.78 = bf16[16,256,192]{1,2,0:T(8,128)(2,1)S(1)} copy(bf16[16,256,192]{2,0,1:T(8,128)(2,1)} %bitcast.136) | data formatting | bytes 3145728 | tf_op jit(solution)/shard_map/optimization_barrier | solution.py:155
  184.8 3.7 %convolution_convert_fusion.1 = bf16[16,256,576]{1,2,0:T(8,128)(2,1)} fusion(bf16[16,256,192]{1,2,0:T(8,128)(2,1)S(1)} %copy.78, f32[192]{0:T(256)S(1)} %copy-done.14, f32[16,256]{1,0:T(8,128)S(1)} %add_rsqrt_fusion.3, f32[16,256]{1,0:T(8,128)S(1)} %broadcast_multiply_fusion.3, bf16[192,576]{1,0:T(8,128)(2,1)S(1)} %copy-done.10), kind=kOutput, calls=%fused_computation.79 | convolution fusion | flops 912261120 | bytes 6546176 | tf_op jit(solution)/shard_map/dot_general | solution.py:30
  188.5 14.5 %fusion.125 = (f32[16,6,256]{2,1,0:T(8,128)S(1)}, f32[16,6,256,256]{2,3,1,0:T(8,128)}) fusion(bf16[16,256,3,6,32]{1,4,3,2,0:T(8,128)(2,1)} %bitcast.146), kind=kOutput, calls=%fused_computation.171 | convolution fusion | flops 421527808 | bytes 28409856 | tf_op jit(solution)/shard_map/sub | solution.py:46
  203.1 10.9 %fusion.69 = bf16[16,6,32,256]{3,2,1,0:T(8,128)(2,1)S(1)} fusion(f32[16,6,256,256]{2,3,1,0:T(8,128)} %get-tuple-element.33, f32[16,6,256]{2,1,0:T(8,128)S(1)} %broadcast_divide_fusion.1, bf16[16,256,3,6,32]{1,4,3,2,0:T(8,128)(2,1)} %bitcast.147), kind=kOutput, calls=%fused_computation.89 | convolution fusion | flops 416022528 | bytes 28409856 | tf_op jit(solution)/shard_map/ghts,gshd->gthd/dot_general | solution.py:49
  214.0 0.8 convert_reduce_fusion.2
  215.3 7.0 %fusion.50 = bf16[16,256,192]{1,2,0:T(8,128)(2,1)} fusion(bf16[16,256,192]{1,2,0:T(8,128)(2,1)S(1)} %get-tuple-element.35, f32[192]{0:T(256)S(1)} %copy-done.15, f32[16,256]{1,0:T(8,128)S(1)} %add_rsqrt_fusion.2, f32[16,256]{1,0:T(8,128)S(1)} %broadcast_multiply_fusion.2, bf16[768,192]{0,1:T(8,128)(2,1)} %param.33, bf16[192,768]{1,0:T(8,128)(2,1)} %param.32), kind=kOutput, calls=%fused_computation.73 | convolution fusion | flops 2437939200 | bytes 3769088 | tf_op jit(solution)/shard_map/dot_general | solution.py:30
  222.3 3.2 %copy.84 = bf16[16,256,192]{2,0,1:T(8,128)(2,1)S(1)} copy(bf16[16,256,192]{1,2,0:T(8,128)(2,1)} %fusion.50) | data formatting | bytes 3145728 | tf_op jit(solution)/shard_map/convert_element_type | solution.py:59
  225.5 2.9 %copy.85 = bf16[128,2,8,2,192]{0,4,3,2,1:T(8,128)(2,1)} copy(bf16[128,2,8,2,192]{4,2,1,3,0:T(8,128)(2,1)S(1)} %bitcast.137) | data formatting | bytes 3145728 | tf_op jit(solution)/shard_map/transpose | solution.py:160
  228.5 2.0 copy.86
  230.5 29.0 %all_to_all.11 = bf16[128,48,128]{2,1,0:T(8,128)(2,1)} all-to-all(bf16[128,48,128]{2,1,0:T(8,128)(2,1)S(1)} %copy.86), channel_id=1, replica_groups=mesh['rows'=16,'cols'=8] {'rows','cols'}, dimensions={0} | all-to-all | bytes 3145728 | tf_op jit(solution)/shard_map/all_to_all | solution.py:161
  259.5 5.1 %reshape.172 = bf16[16,8,2,8,1,2,192]{6,5,3,2,1,0,4:T(2,128)(2,1)S(1)} reshape(bf16[128,48,128]{2,1,0:T(8,128)(2,1)} %all_to_all.11) | data formatting | bytes 3145728 | tf_op jit(solution)/shard_map/reshape | solution.py:163
  264.7 1.8 copy.87
  266.4 3.9 %copy.88 = bf16[32,128,192]{1,2,0:T(8,128)(2,1)} copy(bf16[32,128,192]{2,1,0:T(8,128)(2,1)} %bitcast.140) | data formatting | bytes 3145728 | tf_op jit(solution)/shard_map/reshape | solution.py:167
  (63 shorter events, 3.9 us)
Async XLA Ops:
  0.0 12.8 %copy-start = (bf16[192,768]{1,0:T(8,128)(2,1)S(1)}, bf16[192,768]{1,0:T(8,128)(2,1)}, u32[]{:S(2)}) copy-start(bf16[192,768]{1,0:T(8,128)(2,1)} %param.19) | copy-start | bytes 884740
  1.6 21.7 %collective-permute-start.1 = (bf16[128,192]{1,0:T(8,128)(2,1)}, bf16[128,192]{1,0:T(8,128)(2,1)S(1)}, u32[]{:S(2)}, u32[]{:S(2)}) collective-permute-start(bf16[128,192]{1,0:T(8,128)(2,1)} %bitcast.1), channel_id=1, source_target_pairs={{8,0},{16,8},{24,16},{32,24},{40,32},{48,40},{56,48},{64,56},{72,6... | collective-permute-start | bytes 147464 | tf_op jit(solution)/shard_map/ppermute | solution.py:96
  5.6 17.7 %collective-permute-start = (bf16[128,192]{1,0:T(8,128)(2,1)}, bf16[128,192]{1,0:T(8,128)(2,1)}, u32[]{:S(2)}, u32[]{:S(2)}) collective-permute-start(bf16[128,192]{1,0:T(8,128)(2,1)} %bitcast), channel_id=1, source_target_pairs={{0,8},{8,16},{16,24},{24,32},{32,40},{40,48},{48,56},{56,64},{64,7... | collective-permute-start | bytes 147464 | tf_op jit(solution)/shard_map/ppermute | solution.py:95
  12.8 5.9 %copy-start.2 = (bf16[32,128,192]{1,2,0:T(8,128)(2,1)S(1)}, bf16[32,128,192]{1,2,0:T(8,128)(2,1)}, u32[]{:S(2)}) copy-start(bf16[32,128,192]{1,2,0:T(8,128)(2,1)} %param.17) | copy-start | bytes 4718596
  18.7 16.0 %copy-start.11 = (f32[192]{0:T(256)S(1)}, f32[192]{0:T(256)}, u32[]{:S(2)}) copy-start(f32[192]{0:T(256)} %param.18) | copy-start | bytes 2308
  24.0 8.6 %collective-permute-start.3 = (bf16[34,192]{1,0:T(8,128)(2,1)S(1)}, bf16[34,192]{1,0:T(8,128)(2,1)S(1)}, u32[]{:S(2)}, u32[]{:S(2)}) collective-permute-start(bf16[34,192]{1,0:T(8,128)(2,1)S(1)} %pad_maximum_fusion.5), channel_id=1, source_target_pairs={{1,0},{2,1},{3,2},{4,3},{5,4},{6,5},{7,6},{9,8},{10,9},{11,10},{12... | collective-permute-start | bytes 39176 | tf_op jit(solution)/shard_map/ppermute | solution.py:102
  25.4 7.3 %collective-permute-start.2 = (bf16[34,192]{1,0:T(8,128)(2,1)S(1)}, bf16[34,192]{1,0:T(8,128)(2,1)S(1)}, u32[]{:S(2)}, u32[]{:S(2)}) collective-permute-start(bf16[34,192]{1,0:T(8,128)(2,1)S(1)} %pad_maximum_fusion.4), channel_id=1, source_target_pairs={{0,1},{1,2},{2,3},{3,4},{4,5},{5,6},{6,7},{8,9},{9,10},{10,11},{11... | collective-permute-start | bytes 39176 | tf_op jit(solution)/shard_map/ppermute | solution.py:101
  36.3 10.1 %copy-start.6 = (bf16[768,192]{0,1:T(8,128)(2,1)S(1)}, bf16[768,192]{0,1:T(8,128)(2,1)}, u32[]{:S(2)}) copy-start(bf16[768,192]{0,1:T(8,128)(2,1)} %param.21) | copy-start | bytes 884740
  71.0 3.9 %copy-start.9 = (bf16[192,576]{1,0:T(8,128)(2,1)S(1)}, bf16[192,576]{1,0:T(8,128)(2,1)}, u32[]{:S(2)}) copy-start(bf16[192,576]{1,0:T(8,128)(2,1)} %param.23) | copy-start | bytes 663556
  71.0 3.9 %copy-start.12 = (f32[192]{0:T(256)S(1)}, f32[192]{0:T(256)}, u32[]{:S(2)}) copy-start(f32[192]{0:T(256)} %param.22) | copy-start | bytes 2308
  115.0 7.3 %copy-start.4 = (bf16[192,192]{1,0:T(8,128)(2,1)S(1)}, bf16[192,192]{1,0:T(8,128)(2,1)}, u32[]{:S(2)}) copy-start(bf16[192,192]{1,0:T(8,128)(2,1)} %param.24) | copy-start | bytes 221188
  122.3 4.4 %copy-start.7 = (bf16[768,192]{0,1:T(8,128)(2,1)S(1)}, bf16[768,192]{0,1:T(8,128)(2,1)}, u32[]{:S(2)}) copy-start(bf16[768,192]{0,1:T(8,128)(2,1)} %param.27) | copy-start | bytes 884740
  122.3 4.4 %copy-start.8 = (bf16[192,768]{1,0:T(8,128)(2,1)S(1)}, bf16[192,768]{1,0:T(8,128)(2,1)}, u32[]{:S(2)}) copy-start(bf16[192,768]{1,0:T(8,128)(2,1)} %param.26) | copy-start | bytes 884740
  122.3 4.4 %copy-start.13 = (f32[192]{0:T(256)S(1)}, f32[192]{0:T(256)}, u32[]{:S(2)}) copy-start(f32[192]{0:T(256)} %param.25) | copy-start | bytes 2308
  124.0 1.4 copy-start.3
  177.6 7.2 %copy-start.10 = (bf16[192,576]{1,0:T(8,128)(2,1)S(1)}, bf16[192,576]{1,0:T(8,128)(2,1)}, u32[]{:S(2)}) copy-start(bf16[192,576]{1,0:T(8,128)(2,1)} %param.29) | copy-start | bytes 663556
  177.6 7.2 %copy-start.14 = (f32[192]{0:T(256)S(1)}, f32[192]{0:T(256)}, u32[]{:S(2)}) copy-start(f32[192]{0:T(256)} %param.28) | copy-start | bytes 2308
  203.1 10.9 %copy-start.5 = (bf16[192,192]{1,0:T(8,128)(2,1)S(1)}, bf16[192,192]{1,0:T(8,128)(2,1)}, u32[]{:S(2)}) copy-start(bf16[192,192]{1,0:T(8,128)(2,1)} %param.30) | copy-start | bytes 221188
  214.0 1.3 copy-start.15
  259.5 10.8 %copy-start.1 = (bf16[192,768]{1,0:T(8,128)(2,1)S(1)}, bf16[192,768]{1,0:T(8,128)(2,1)}, u32[]{:S(2)}) copy-start(bf16[192,768]{1,0:T(8,128)(2,1)} %param.19) | copy-start | bytes 884740

commit v2 on v1

--- a/solution.py
+++ b/solution.py
@@ -34,21 +34,22 @@
 def attend(normed, w_qkv, w_out):
     groups, tokens, channels = normed.shape
     head_size = channels // HEADS
-    qkv_all = project(normed, w_qkv).astype(jnp.bfloat16)
-    heads_split = qkv_all.reshape(groups, tokens, 3, HEADS, head_size)
+    w_split = w_qkv.reshape(channels, 3, HEADS, head_size)
+
+    def heads_of(part):
+        return jnp.einsum(
+            "gtc,chd->ghtd", normed, w_split[:, part], preferred_element_type=jnp.float32
+        ).astype(jnp.bfloat16)
+
+    queries, keys, values = heads_of(0), heads_of(1), heads_of(2)
     scores = jnp.einsum(
-        "gthd,gshd->ghts",
-        heads_split[:, :, 0],
-        heads_split[:, :, 1],
-        preferred_element_type=jnp.float32,
+        "ghtd,ghsd->ghts", queries, keys, preferred_element_type=jnp.float32
     ) * head_size ** (-0.5)
     peak = jnp.max(scores, axis=-1, keepdims=True)
     lifted = jnp.exp(scores - peak)
     total = jnp.sum(lifted, axis=-1, keepdims=True)
     weights = (lifted * (1.0 / total)).astype(jnp.bfloat16)
-    mixed = jnp.einsum(
-        "ghts,gshd->gthd", weights, heads_split[:, :, 2], preferred_element_type=jnp.float32
-    )
+    mixed = jnp.einsum("ghts,ghsd->gthd", weights, values, preferred_element_type=jnp.float32)
     mixed = mixed.astype(jnp.bfloat16).reshape(groups, tokens, channels)
     return project(mixed, w_out)
 
@@ -129,11 +130,6 @@
     update = attend(layer_norm(windows, gain_block), qkv_block, out_block)
     mixed_after = (windows.astype(jnp.float32) + update).astype(jnp.bfloat16)
     mixed_after = feed_forward(mixed_after, gain_bffn, ffn_in_block, ffn_out_block)
-    block_out = (
-        mixed_after.reshape(win_rows, win_cols, BLOCK, BLOCK, channels)
-        .transpose(0, 2, 1, 3, 4)
-        .reshape(tile_rows, tile_cols, channels)
-    )
     local_rows = G // rows_count
     local_cols = G // cols_count
     stride_rows = tile_rows // local_rows
@@ -141,9 +137,17 @@
     part_rows = stride_rows // rows_count
     part_cols = stride_cols // cols_count
     devices = rows_count * cols_count
-    split = block_out.reshape(
-        local_rows, rows_count, part_rows, local_cols, cols_count, part_cols, channels
-    ).transpose(1, 4, 2, 5, 0, 3, 6)
+    assert part_cols == BLOCK and BLOCK % part_rows == 0
+    split = mixed_after.reshape(
+        local_rows,
+        win_rows // local_rows,
+        local_cols,
+        cols_count,
+        BLOCK // part_rows,
+        part_rows,
+        BLOCK,
+        channels,
+    ).transpose(1, 4, 3, 5, 6, 0, 2, 7)
     piece = (part_rows, part_cols, local_rows * local_cols, channels)
     packed = split.reshape(devices, -1, 128)
     received = lax.all_to_all(packed, both, split_axis=0, concat_axis=0, tiled=True)

time: 275 us -> 265 us (0.964)
  blocking collectives: 65.8 us -> 29 us
  waiting for transfers between devices: 0.01 us -> 24.8 us
  starting transfers between devices: 14.5 us -> 25.9 us
  local copies, waits for them, and re-layouts: 57.2 us -> 51.3 us
  matrix products: 94.6 us -> 91.1 us
    all_to_all x2 -> x1, blocking collectives: 65.8 us -> 29 us  [shards_body(): lax.all_to_all(packed, both, split_axis=0, concat_axis=0, tiled=True)]
    all_to_all x0 -> x1, waiting for transfers between devices: none -> 24.8 us  [shards_body(): lax.all_to_all(packed, both, split_axis=0, concat_axis=0, tiled=True)]
    all_to_all x0 -> x1, starting transfers between devices: none -> 11.4 us  [shards_body(): lax.all_to_all(packed, both, split_axis=0, concat_axis=0, tiled=True)]
    convert_element_type x1 -> x0, local copies, waits for them, and re-layouts: 10.2 us -> none  [attend(): qkv_all = project(normed, w_qkv).astype(jnp.bfloat16)]
    dot_general x9 -> x7, matrix products: 52.7 us -> 48.1 us  [project(): output = jnp.dot(flattened, weight, preferred_element_type=jnp.float32)]
    reshape x1, local copies, waits for them, and re-layouts: 0.25 us -> 4.83 us  [shards_body(): mixed_after.reshape(local_rows, win_rows // local_rows, local_cols, cols_...]
    transpose x1 -> x0, local copies, waits for them, and re-layouts: 3.29 us -> none  [shards_body(): split = block_out.reshape(local_rows, rows_count, part_rows, local_cols,...]
    unnamed x36 -> x42, local copies, waits for them, and re-layouts: 5.63 us -> 8.73 us
  transfers between devices with their start and end apart: 4 -> 5, of which waited for: 0 -> 1; matrix products, arithmetic and copies ran while one was open for 6% -> 7% of each run, Pallas kernels for 0% -> 0%
where the time goes in v2:
time: 265 us; the launch traced here: 261 us
  matrix products  91.1 us (34%)
  local copies, waits for them, and re-layouts  51.3 us (19%)
  other arithmetic  37.6 us (14%)
  blocking collectives  29 us (11%)
  starting transfers between devices  25.9 us (10%)
  waiting for transfers between devices  24.8 us (9%)
    dot_general x7, matrix products, project(): output = jnp.dot(flattened, weight, preferred_element_type=jnp.float32)  48.1 us
    all_to_all x1, blocking collectives, shards_body(): lax.all_to_all(packed, both, split_axis=0, concat_axis=0, tiled=True)  29 us
    all_to_all x1, waiting for transfers between devices, shards_body(): lax.all_to_all(packed, both, split_axis=0, concat_axis=0, tiled=True)  24.8 us
    dot_general x2, matrix products, attend(): jnp.einsum('ghts,ghsd->gthd', weights, values, preferred_element_type=jnp...  18.6 us
    sub x1, other arithmetic, attend(): lifted = jnp.exp(scores - peak)  16.4 us
    sub x1, matrix products, attend(): lifted = jnp.exp(scores - peak)  14.1 us
    all_to_all x1, starting transfers between devices, shards_body(): lax.all_to_all(packed, both, split_axis=0, concat_axis=0, tiled=True)  11.4 us
    concatenate x1, other arithmetic, shards_body(): expanded = jnp.concatenate([left, expanded, right], axis=1)  10.1 us
  transfers between devices with their start and end apart: 5, of which 1 were waited for; matrix products, arithmetic and copies ran while one was open for 7% of the time, Pallas kernels for 0%

profile of v2, /device:TPU:1, one launch (start us, length us, event | category | flops | bytes accessed | tf_op | source)
XLA Modules:
  0.0 260.7 jit_solution(8381581716776991985)
XLA Ops:
  0.0 0.9 fusion.147
  0.9 0.7 copy.79
  1.6 3.3 %collective-permute-start.1 = (bf16[128,192]{1,0:T(8,128)(2,1)}, bf16[128,192]{1,0:T(8,128)(2,1)S(1)}, u32[]{:S(2)}, u32[]{:S(2)}) collective-permute-start(bf16[128,192]{1,0:T(8,128)(2,1)} %bitcast.1), channel_id=1, source_target_pairs={{8,0},{16,8},{24,16},{32,24},{40,32},{48,40},{56,48},{64,56},{72,6... | collective-permute-start | bytes 147464 | tf_op jit(solution)/shard_map/ppermute | solution.py:97
  5.6 3.5 %collective-permute-start = (bf16[128,192]{1,0:T(8,128)(2,1)}, bf16[128,192]{1,0:T(8,128)(2,1)}, u32[]{:S(2)}, u32[]{:S(2)}) collective-permute-start(bf16[128,192]{1,0:T(8,128)(2,1)} %bitcast), channel_id=1, source_target_pairs={{0,8},{8,16},{16,24},{24,32},{32,40},{40,48},{48,56},{56,64},{64,7... | collective-permute-start | bytes 147464 | tf_op jit(solution)/shard_map/ppermute | solution.py:96
  9.2 1.7 convert_reduce_fusion.4
  10.9 1.9 fusion.45
  12.8 5.9 %multiply_convert_fusion.6 = bf16[32,128,768]{2,1,0:T(8,128)(2,1)} fusion(bf16[32,128,192]{1,2,0:T(8,128)(2,1)} %param.17, f32[192]{0:T(256)} %param.18, f32[32,128]{1,0:T(8,128)S(1)} %add_rsqrt_fusion.4, f32[32,128]{1,0:T(8,128)S(1)} %broadcast_multiply_fusion.4, bf16[192,768]{1,0:T(8,128)(2,1)S(1)} %copy-done), kind=kOutput, calls=%fused_computation.14 | convolution fusion | flops 1227620352 | bytes 8192768 | tf_op jit(solution)/shard_map/dot_general | solution.py:30
  18.7 1.8 fusion.146
  20.5 1.9 copy.80
  22.4 0.9 copy.81
  24.0 1.3 collective-permute-start.3
  25.4 6.4 %collective-permute-start.2 = (bf16[34,192]{1,0:T(8,128)(2,1)S(1)}, bf16[34,192]{1,0:T(8,128)(2,1)S(1)}, u32[]{:S(2)}, u32[]{:S(2)}) collective-permute-start(bf16[34,192]{1,0:T(8,128)(2,1)S(1)} %pad_maximum_fusion.4), channel_id=1, source_target_pairs={{0,1},{1,2},{2,3},{3,4},{4,5},{5,6},{6,7},{8,9},{9,10},{10,11},{11... | collective-permute-start | bytes 39176 | tf_op jit(solution)/shard_map/ppermute | solution.py:102
  31.7 0.9 convert_reduce_fusion.14
  32.7 1.8 copy.56
  34.5 1.0 convert_reduce_fusion.5
  35.5 1.1 fusion.113
  36.6 1.2 multiply_convert_fusion.21
  38.1 10.1 %maximum_maximum_fusion = (bf16[34,129,768]{2,1,0:T(8,128)(2,1)S(1)}, bf16[34,129,768]{2,1,0:T(8,128)(2,1)S(1)}) fusion(bf16[1,128,768]{2,1,0:T(8,128)(2,1)S(1)} %get-tuple-element.23, bf16[32,128,768]{2,1,0:T(8,128)(2,1)} %multiply_convert_fusion.6, bf16[1,128,768]{2,1,0:T(8,128)(2,1)S(1)} %get-tuple-element.22, bf16[34,1,768]{2,1,0:T(2,128)(2,1)S(1)} %copy.52, ...), kind=kLoop, calls=%fused_computation.17 | loop fusion | flops 53895168 | bytes 20262912 | tf_op jit(solution)/shard_map/concatenate | solution.py:113
  48.2 21.9 %fusion.48 = bf16[32,128,192]{1,2,0:T(8,128)(2,1)S(1)} fusion(bf16[32,128,192]{1,2,0:T(8,128)(2,1)S(1)} %copy-done.2, bf16[32,128,768]{2,1,0:T(8,128)(2,1)} %multiply_convert_fusion.6, bf16[34,129,768]{2,1,0:T(8,128)(2,1)S(1)} %get-tuple-element.15, bf16[1,128,768]{2,1,0:T(8,128)(2,1)S(1)} %get-tuple-element.23, ...), kind=kOutput, calls=%fused_computation.71 | convolution fusion | flops 1326710784 | bytes 47910912 | tf_op jit(solution)/shard_map/dot_general | solution.py:30
  70.1 2.6 %copy.54 = bf16[32,128,192]{2,1,0:T(8,128)(2,1)} copy(bf16[32,128,192]{1,2,0:T(8,128)(2,1)S(1)} %fusion.48) | data formatting | bytes 3145728 | tf_op jit(solution)/shard_map/convert_element_type | solution.py:121
  72.7 1.9 copy.55
  75.3 1.3 fusion.24
  76.6 7.7 %fusion.51 = f32[64,6,64,64]{2,3,1,0:T(8,128)} fusion(bf16[64,64,192]{2,1,0:T(8,128)(2,1)S(1)} %bitcast.158, f32[192]{0:T(256)S(1)} %copy-done.10, f32[64,64]{1,0:T(8,128)S(1)} %add_rsqrt_fusion.1, f32[64,64]{1,0:T(8,128)S(1)} %broadcast_multiply_fusion.1, bf16[192,3,6,32]{0,3,2,1:T(8,128)(2,1)S(1)} %bitcast.172), kind=kOutput, calls=%fused_computation.74 | convolution fusion | flops 714080256 | bytes 10815488 | tf_op jit(solution)/shard_map/ghtd,ghsd->ghts/dot_general | solution.py:45
  84.3 16.4 %fusion.150 = (f32[64,6,64]{2,1,0:T(8,128)S(1)}, f32[64,6,64,64]{2,3,1,0:T(8,128)}) fusion(f32[64,6,64,64]{2,3,1,0:T(8,128)} %fusion.51), kind=kOutput, calls=%fused_computation.180 | output fusion | flops 6291519 | bytes 12681216 | tf_op jit(solution)/shard_map/sub | solution.py:49
  100.8 7.5 %fusion.64 = bf16[64,6,32,64]{3,2,1,0:T(8,128)(2,1)} fusion(f32[64,6,64,64]{2,3,1,0:T(8,128)} %get-tuple-element.29, f32[64,6,64]{2,1,0:T(8,128)S(1)} %broadcast_divide_fusion, bf16[64,64,192]{2,1,0:T(8,128)(2,1)S(1)} %bitcast.159, f32[192]{0:T(256)S(1)} %copy-done.10, f32[64,64]{1,0:T(8,128)S(1)} %add_rsqrt_fusion.1, ...), kind=kOutput, calls=%fused_computation.84 | convolution fusion | flops 411303936 | bytes 10388480 | tf_op jit(solution)/shard_map/ghts,ghsd->gthd/dot_general | solution.py:52
  108.3 3.6 %convert_reduce_fusion = (f32[64,64]{1,0:T(8,128)S(1)}, bf16[64,64,192]{2,1,0:T(8,128)(2,1)S(1)}) fusion(bf16[64,64,192]{1,2,0:T(8,128)(2,1)} %bitcast.161, bf16[192,192]{1,0:T(8,128)(2,1)S(1)} %copy-done.8, bf16[64,64,192]{2,1,0:T(8,128)(2,1)S(1)} %bitcast.160), kind=kOutput, calls=%fused_computation.24 | convolution fusion | flops 305917952 | bytes 4808704 | tf_op jit(solution)/shard_map/dot_general | solution.py:30
  111.9 1.3 copy-done.3
  113.3 1.3 fusion.21
  114.7 7.1 %fusion.28 = bf16[64,64,192]{2,1,0:T(8,128)(2,1)} fusion(bf16[64,64,192]{2,1,0:T(8,128)(2,1)} %copy-done.3, f32[192]{0:T(256)S(1)} %copy-done.16, f32[64,64]{1,0:T(8,128)S(1)} %add_rsqrt_fusion, f32[64,64]{1,0:T(8,128)S(1)} %broadcast_multiply_fusion, bf16[768,192]{0,1:T(8,128)(2,1)S(1)} %copy-done.13, bf16[192,768]{1,0:T(8,128)(2,1)S(1)} %copy-done.14), kind=kOutput, calls=%fused_computation.53 | convolution fusion | flops 2437939200 | bytes 3769088 | tf_op jit(solution)/shard_map/dot_general | solution.py:30
  121.7 4.8 %copy.83 = bf16[1,4,2,8,4,2,8,192]{7,2,6,5,3,4,1,0:T(2,128)(2,1)S(1)} copy(bf16[1,4,2,8,4,2,8,192]{7,6,5,4,3,2,1,0:T(8,128)(2,1)} %bitcast.171) | data formatting | bytes 3145728 | tf_op jit(solution)/shard_map/reshape | solution.py:141
  126.6 3.0 %reshape.158 = bf16[128,48,128]{2,1,0:T(8,128)(2,1)} reshape(bf16[4,4,8,2,8,1,2,192]{7,6,4,3,2,1,0,5:T(2,128)(2,1)S(1)} %bitcast.165) | data formatting | bytes 3145728 | tf_op jit(solution)/shard_map/reshape | solution.py:152
  129.6 11.4 %all-to-all-start = ((bf16[128,48,128]{2,1,0:T(8,128)(2,1)}), bf16[128,48,128]{2,1,0:T(8,128)(2,1)S(1)}, u32[]{:S(2)}, u32[]{:S(2)}) async-start(bf16[128,48,128]{2,1,0:T(8,128)(2,1)} %reshape.158), calls=%async_computation | async-start | bytes 3145728 | tf_op jit(solution)/shard_map/all_to_all | solution.py:153
  141.2 24.8 %all-to-all-done = bf16[128,48,128]{2,1,0:T(8,128)(2,1)S(1)} async-done(((bf16[128,48,128]{2,1,0:T(8,128)(2,1)}), bf16[128,48,128]{2,1,0:T(8,128)(2,1)S(1)}, u32[]{:S(2)}, u32[]{:S(2)}) %all-to-all-start) | async-done | bytes 1572896 | tf_op jit(solution)/shard_map/all_to_all | solution.py:153
  166.0 1.1 copy.60
  167.1 3.0 %copy.61 = bf16[2,8,128,2,192]{4,1,0,3,2:T(8,128)(2,1)} copy(bf16[2,8,128,2,192]{2,4,3,1,0:T(8,128)(2,1)S(1)} %bitcast.169) | data formatting | bytes 3145728 | tf_op jit(solution)/shard_map/transpose | solution.py:156
  170.1 3.5 %copy.62 = bf16[16,256,192]{1,2,0:T(8,128)(2,1)S(1)} copy(bf16[16,256,192]{2,0,1:T(8,128)(2,1)} %bitcast.162) | data formatting | bytes 3145728 | tf_op jit(solution)/shard_map/optimization_barrier | solution.py:159
  175.1 1.8 convolution_convert_fusion.1
  176.9 14.1 %fusion.151 = (f32[16,6,256]{2,1,0:T(8,128)S(1)}, f32[16,6,256,256]{2,3,1,0:T(8,128)}) fusion(bf16[16,256,6,32]{1,3,2,0:T(8,128)(2,1)} %convolution_convert_fusion.1, bf16[16,256,6,32]{1,3,2,0:T(8,128)(2,1)S(1)} %convolution_convert_fusion.2), kind=kOutput, calls=%fused_computation.181 | convolution fusion | flops 421527808 | bytes 28409856 | tf_op jit(solution)/shard_map/sub | solution.py:49
  191.1 11.1 %fusion.80 = bf16[16,6,32,256]{3,2,1,0:T(8,128)(2,1)S(1)} fusion(f32[16,6,256,256]{2,3,1,0:T(8,128)} %get-tuple-element.33, f32[16,6,256]{2,1,0:T(8,128)S(1)} %broadcast_divide_fusion.1, bf16[192,3,6,32]{0,3,2,1:T(8,128)(2,1)} %bitcast.176, bf16[16,256,192]{1,2,0:T(8,128)(2,1)S(1)} %copy.62, f32[192]{0:T(256)S(1)} %copy-done.11, ...), kind=kOutput, calls=%fused_computation.95 | convolution fusion | flops 722731008 | bytes 28541696 | tf_op jit(solution)/shard_map/ghts,ghsd->gthd/dot_general | solution.py:52
  203.0 1.1 copy-done.4
  204.5 7.7 %fusion.50 = bf16[16,256,192]{1,2,0:T(8,128)(2,1)} fusion(bf16[16,256,192]{1,2,0:T(8,128)(2,1)} %copy-done.4, f32[192]{0:T(256)S(1)} %copy-done.17, f32[16,256]{1,0:T(8,128)S(1)} %add_rsqrt_fusion.2, f32[16,256]{1,0:T(8,128)S(1)} %broadcast_multiply_fusion.2, bf16[768,192]{0,1:T(8,128)(2,1)} %param.33, bf16[192,768]{1,0:T(8,128)(2,1)} %param.32), kind=kOutput, calls=%fused_computation.73 | convolution fusion | flops 2437939200 | bytes 3769088 | tf_op jit(solution)/shard_map/dot_general | solution.py:30
  212.2 3.2 %copy.66 = bf16[16,256,192]{2,0,1:T(8,128)(2,1)S(1)} copy(bf16[16,256,192]{1,2,0:T(8,128)(2,1)} %fusion.50) | data formatting | bytes 3145728 | tf_op jit(solution)/shard_map/convert_element_type | solution.py:60
  215.5 2.9 %copy.67 = bf16[128,2,8,2,192]{0,4,3,2,1:T(8,128)(2,1)} copy(bf16[128,2,8,2,192]{4,2,1,3,0:T(8,128)(2,1)S(1)} %bitcast.163) | data formatting | bytes 3145728 | tf_op jit(solution)/shard_map/transpose | solution.py:164
  218.4 2.0 copy.68
  220.4 29.0 %all_to_all.10 = bf16[128,48,128]{2,1,0:T(8,128)(2,1)} all-to-all(bf16[128,48,128]{2,1,0:T(8,128)(2,1)S(1)} %copy.68), channel_id=1, replica_groups=mesh['rows'=16,'cols'=8] {'rows','cols'}, dimensions={0} | all-to-all | bytes 3145728 | tf_op jit(solution)/shard_map/all_to_all | solution.py:165
  249.5 5.1 %reshape.164 = bf16[16,8,2,8,1,2,192]{6,5,3,2,1,0,4:T(2,128)(2,1)S(1)} reshape(bf16[128,48,128]{2,1,0:T(8,128)(2,1)} %all_to_all.10) | data formatting | bytes 3145728 | tf_op jit(solution)/shard_map/reshape | solution.py:167
  254.6 1.8 copy.69
  256.4 3.9 %copy.70 = bf16[32,128,192]{1,2,0:T(8,128)(2,1)} copy(bf16[32,128,192]{2,1,0:T(8,128)(2,1)} %bitcast.167) | data formatting | bytes 3145728 | tf_op jit(solution)/shard_map/reshape | solution.py:171
  (68 shorter events, 5.2 us)
Async XLA Ops:
  0.0 12.8 %copy-start = (bf16[192,768]{1,0:T(8,128)(2,1)S(1)}, bf16[192,768]{1,0:T(8,128)(2,1)}, u32[]{:S(2)}) copy-start(bf16[192,768]{1,0:T(8,128)(2,1)} %param.19) | copy-start | bytes 884740
  1.6 21.7 %collective-permute-start.1 = (bf16[128,192]{1,0:T(8,128)(2,1)}, bf16[128,192]{1,0:T(8,128)(2,1)S(1)}, u32[]{:S(2)}, u32[]{:S(2)}) collective-permute-start(bf16[128,192]{1,0:T(8,128)(2,1)} %bitcast.1), channel_id=1, source_target_pairs={{8,0},{16,8},{24,16},{32,24},{40,32},{48,40},{56,48},{64,56},{72,6... | collective-permute-start | bytes 147464 | tf_op jit(solution)/shard_map/ppermute | solution.py:97
  5.6 17.7 %collective-permute-start = (bf16[128,192]{1,0:T(8,128)(2,1)}, bf16[128,192]{1,0:T(8,128)(2,1)}, u32[]{:S(2)}, u32[]{:S(2)}) collective-permute-start(bf16[128,192]{1,0:T(8,128)(2,1)} %bitcast), channel_id=1, source_target_pairs={{0,8},{8,16},{16,24},{24,32},{32,40},{40,48},{48,56},{56,64},{64,7... | collective-permute-start | bytes 147464 | tf_op jit(solution)/shard_map/ppermute | solution.py:96
  12.8 5.9 %copy-start.2 = (bf16[32,128,192]{1,2,0:T(8,128)(2,1)S(1)}, bf16[32,128,192]{1,2,0:T(8,128)(2,1)}, u32[]{:S(2)}) copy-start(bf16[32,128,192]{1,2,0:T(8,128)(2,1)} %param.17) | copy-start | bytes 4718596
  18.7 17.8 %copy-start.15 = (f32[192]{0:T(256)S(1)}, f32[192]{0:T(256)}, u32[]{:S(2)}) copy-start(f32[192]{0:T(256)} %param.18) | copy-start | bytes 2308
  24.0 10.4 %collective-permute-start.3 = (bf16[34,192]{1,0:T(8,128)(2,1)S(1)}, bf16[34,192]{1,0:T(8,128)(2,1)S(1)}, u32[]{:S(2)}, u32[]{:S(2)}) collective-permute-start(bf16[34,192]{1,0:T(8,128)(2,1)S(1)} %pad_maximum_fusion.5), channel_id=1, source_target_pairs={{1,0},{2,1},{3,2},{4,3},{5,4},{6,5},{7,6},{9,8},{10,9},{11,10},{12... | collective-permute-start | bytes 39176 | tf_op jit(solution)/shard_map/ppermute | solution.py:103
  25.4 9.1 %collective-permute-start.2 = (bf16[34,192]{1,0:T(8,128)(2,1)S(1)}, bf16[34,192]{1,0:T(8,128)(2,1)S(1)}, u32[]{:S(2)}, u32[]{:S(2)}) collective-permute-start(bf16[34,192]{1,0:T(8,128)(2,1)S(1)} %pad_maximum_fusion.4), channel_id=1, source_target_pairs={{0,1},{1,2},{2,3},{3,4},{4,5},{5,6},{6,7},{8,9},{9,10},{10,11},{11... | collective-permute-start | bytes 39176 | tf_op jit(solution)/shard_map/ppermute | solution.py:102
  38.1 10.1 %copy-start.12 = (bf16[768,192]{0,1:T(8,128)(2,1)S(1)}, bf16[768,192]{0,1:T(8,128)(2,1)}, u32[]{:S(2)}) copy-start(bf16[768,192]{0,1:T(8,128)(2,1)} %param.21) | copy-start | bytes 884740
  72.7 3.9 %copy-start.5 = (bf16[192,576]{0,1:T(8,128)(2,1)S(1)}, bf16[192,576]{0,1:T(8,128)(2,1)}, u32[]{:S(2)}) copy-start(bf16[192,576]{0,1:T(8,128)(2,1)} %copy.56) | copy-start | bytes 663556
  72.7 3.9 %copy-start.10 = (f32[192]{0:T(256)S(1)}, f32[192]{0:T(256)}, u32[]{:S(2)}) copy-start(f32[192]{0:T(256)} %param.22) | copy-start | bytes 2308
  100.8 7.5 %copy-start.8 = (bf16[192,192]{1,0:T(8,128)(2,1)S(1)}, bf16[192,192]{1,0:T(8,128)(2,1)}, u32[]{:S(2)}) copy-start(bf16[192,192]{1,0:T(8,128)(2,1)} %param.24) | copy-start | bytes 221188
  108.3 6.3 %copy-start.13 = (bf16[768,192]{0,1:T(8,128)(2,1)S(1)}, bf16[768,192]{0,1:T(8,128)(2,1)}, u32[]{:S(2)}) copy-start(bf16[768,192]{0,1:T(8,128)(2,1)} %param.27) | copy-start | bytes 884740
  108.3 6.3 %copy-start.14 = (bf16[192,768]{1,0:T(8,128)(2,1)S(1)}, bf16[192,768]{1,0:T(8,128)(2,1)}, u32[]{:S(2)}) copy-start(bf16[192,768]{1,0:T(8,128)(2,1)} %param.26) | copy-start | bytes 884740
  108.3 6.3 %copy-start.16 = (f32[192]{0:T(256)S(1)}, f32[192]{0:T(256)}, u32[]{:S(2)}) copy-start(f32[192]{0:T(256)} %param.25) | copy-start | bytes 2308
  111.9 1.4 copy-start.3
  126.5 14.5 %copy-start.7 = (bf16[192,576]{1,0:T(8,128)(2,1)S(1)}, bf16[192,576]{1,0:T(8,128)(2,1)}, u32[]{:S(2)}) copy-start(bf16[192,576]{1,0:T(8,128)(2,1)} %param.29) | copy-start | bytes 663556
  129.6 36.4 %all-to-all-start = ((bf16[128,48,128]{2,1,0:T(8,128)(2,1)}), bf16[128,48,128]{2,1,0:T(8,128)(2,1)S(1)}, u32[]{:S(2)}, u32[]{:S(2)}) async-start(bf16[128,48,128]{2,1,0:T(8,128)(2,1)} %reshape.158), calls=%async_computation | async-start | bytes 3145728 | tf_op jit(solution)/shard_map/all_to_all | solution.py:153
  141.2 33.9 %copy-start.6 = (bf16[192,576]{0,1:T(8,128)(2,1)}, bf16[192,576]{0,1:T(8,128)(2,1)S(1)}, u32[]{:S(2)}) copy-start(bf16[192,576]{0,1:T(8,128)(2,1)S(1)} %copy.63) | copy-start | bytes 663556
  170.1 4.2 %copy-start.11 = (f32[192]{0:T(256)S(1)}, f32[192]{0:T(256)}, u32[]{:S(2)}) copy-start(f32[192]{0:T(256)} %param.28) | copy-start | bytes 2308
  191.1 11.1 %copy-start.9 = (bf16[192,192]{1,0:T(8,128)(2,1)S(1)}, bf16[192,192]{1,0:T(8,128)(2,1)}, u32[]{:S(2)}) copy-start(bf16[192,192]{1,0:T(8,128)(2,1)} %param.30) | copy-start | bytes 221188
  202.2 2.4 copy-start.17
  202.9 1.1 copy-start.4
  249.5 10.8 %copy-start.1 = (bf16[192,768]{1,0:T(8,128)(2,1)S(1)}, bf16[192,768]{1,0:T(8,128)(2,1)}, u32[]{:S(2)}) copy-start(bf16[192,768]{1,0:T(8,128)(2,1)} %param.19) | copy-start | bytes 884740

commit v3 on v0

--- a/solution.py
+++ b/solution.py
@@ -34,19 +34,31 @@
 def attend(normed, w_qkv, w_out):
     groups, tokens, channels = normed.shape
     head_size = channels // HEADS
-    qkv_all = project(normed, w_qkv).astype(jnp.bfloat16)
-    heads_split = qkv_all.reshape(groups, tokens, 3, HEADS, head_size)
-    scores = jnp.einsum(
-        "gthd,gshd->ghts",
-        heads_split[:, :, 0],
-        heads_split[:, :, 1],
-        preferred_element_type=jnp.float32,
-    ) * head_size ** (-0.5)
-    weights = jax.nn.softmax(scores, axis=-1).astype(jnp.bfloat16)
-    mixed = jnp.einsum(
-        "ghts,gshd->gthd", weights, heads_split[:, :, 2], preferred_element_type=jnp.float32
-    )
-    mixed = mixed.astype(jnp.bfloat16).reshape(groups, tokens, channels)
+    w_split = w_qkv.reshape(channels, 3, HEADS, head_size)
+
+    def heads_of(part):
+        return jnp.einsum(
+            "gtc,chd->ghtd", normed, w_split[:, part], preferred_element_type=jnp.float32
+        ).astype(jnp.bfloat16)
+
+    queries, keys, values = heads_of(0), heads_of(1), heads_of(2)
+
+    def core(chunk):
+        q, k, v = chunk
+        scores = jnp.einsum(
+            "ghtd,ghsd->ghts", q, k, preferred_element_type=jnp.float32
+        ) * head_size ** (-0.5)
+        peak = jnp.max(scores, axis=-1, keepdims=True)
+        lifted = jnp.exp(scores - peak)
+        total = jnp.sum(lifted, axis=-1, keepdims=True)
+        weights = (lifted * (1.0 / total)).astype(jnp.bfloat16)
+        mixed = jnp.einsum("ghts,ghsd->gthd", weights, v, preferred_element_type=jnp.float32)
+        return mixed.astype(jnp.bfloat16)
+
+    chunks = max(1, groups * tokens * tokens // (32 * 64 * 64))
+    split = lambda a: a.reshape((chunks, groups // chunks) + a.shape[1:])
+    mixed = lax.map(core, (split(queries), split(keys), split(values)))
+    mixed = mixed.reshape(groups, tokens, channels)
     return project(mixed, w_out)
 
 

time: 275 us -> 296 us (1.076)
  matrix products: 94.7 us -> 135 us
  blocking collectives: 65.8 us -> 29 us
  waiting for transfers between devices: 0.01 us -> 26.5 us
  other arithmetic: 37.6 us -> 25.1 us
  starting transfers between devices: 14.5 us -> 24.1 us
  local copies, waits for them, and re-layouts: 57.2 us -> 50.4 us
    dot_general x3 -> x26, matrix products: 27.5 us -> 70.8 us  [the longest x10 37.2 us: core(): jnp.einsum('ghts,ghsd->gthd', weights, v, preferred_element_type=jnp.floa...]
    all_to_all x2 -> x1, blocking collectives: 65.8 us -> 29 us  [shards_body(): lax.all_to_all(packed, both, split_axis=0, concat_axis=0, tiled=True)]
    all_to_all x0 -> x1, waiting for transfers between devices: none -> 24.8 us  [shards_body(): lax.all_to_all(packed, both, split_axis=0, concat_axis=0, tiled=True)]
    sub x1 -> x2, other arithmetic: 16.4 us -> 3.85 us  [core(): lifted = jnp.exp(scores - peak)]
    all_to_all x0 -> x1, starting transfers between devices: none -> 10.5 us  [shards_body(): lax.all_to_all(packed, both, split_axis=0, concat_axis=0, tiled=True)]
    convert_element_type x1 -> x0, local copies, waits for them, and re-layouts: 10.2 us -> none  [attend(): qkv_all = project(normed, w_qkv).astype(jnp.bfloat16)]
    dot_general x9 -> x7, matrix products: 52.7 us -> 46.6 us  [project(): output = jnp.dot(flattened, weight, preferred_element_type=jnp.float32)]
    sub x1 -> x8, matrix products: 14.5 us -> 17.5 us  [core(): lifted = jnp.exp(scores - peak)]
  transfers between devices with their start and end apart: 4 -> 5, of which waited for: 0 -> 2; matrix products, arithmetic and copies ran while one was open for 6% -> 6% of each run, Pallas kernels for 0% -> 0%
where the time goes in v3:
time: 296 us; the launch traced here: 292 us
  matrix products  135 us (46%)
  local copies, waits for them, and re-layouts  50.4 us (17%)
  blocking collectives  29 us (10%)
  waiting for transfers between devices  26.5 us (9%)
  other arithmetic  25.1 us (8%)
  starting transfers between devices  24.1 us (8%)
    dot_general x7, matrix products, project(): output = jnp.dot(flattened, weight, preferred_element_type=jnp.float32)  46.6 us
    dot_general x10, matrix products, core(): jnp.einsum('ghts,ghsd->gthd', weights, v, preferred_element_type=jnp.floa...  37.2 us
    all_to_all x1, blocking collectives, shards_body(): lax.all_to_all(packed, both, split_axis=0, concat_axis=0, tiled=True)  29 us
    all_to_all x1, waiting for transfers between devices, shards_body(): lax.all_to_all(packed, both, split_axis=0, concat_axis=0, tiled=True)  24.8 us
    dot_general x10, matrix products, core(): jnp.einsum('ghtd,ghsd->ghts', q, k, preferred_element_type=jnp.float32)  18.9 us
    sub x8, matrix products, core(): lifted = jnp.exp(scores - peak)  17.5 us
    dot_general x6, matrix products, heads_of(): jnp.einsum('gtc,chd->ghtd', normed, w_split[:, part], preferred_element_t...  14.7 us
    all_to_all x1, starting transfers between devices, shards_body(): lax.all_to_all(packed, both, split_axis=0, concat_axis=0, tiled=True)  10.5 us
  transfers between devices with their start and end apart: 5, of which 2 were waited for; matrix products, arithmetic and copies ran while one was open for 6% of the time, Pallas kernels for 0%

profile of v3, /device:TPU:1, one launch (start us, length us, event | category | flops | bytes accessed | tf_op | source)
XLA Modules:
  0.0 291.7 jit_solution(10011178944729593790)
XLA Ops:
  1.7 4.9 %collective-permute-start = (bf16[128,192]{1,0:T(8,128)(2,1)}, bf16[128,192]{1,0:T(8,128)(2,1)S(1)}, u32[]{:S(2)}, u32[]{:S(2)}) collective-permute-start(bf16[128,192]{1,0:T(8,128)(2,1)} %bitcast.10), channel_id=1, source_target_pairs={{0,8},{8,16},{16,24},{24,32},{32,40},{40,48},{48,56},{56,64},{64,7... | collective-permute-start | bytes 147464 | tf_op jit(solution)/shard_map/ppermute | solution.py:104
  12.9 5.0 %multiply_convert_fusion.17 = bf16[32,128,768]{2,1,0:T(8,128)(2,1)} fusion(bf16[32,128,192]{1,2,0:T(8,128)(2,1)S(1)} %copy-done.3, f32[192]{0:T(256)S(1)} %copy-done.15, f32[32,128]{1,0:T(8,128)S(1)} %add_rsqrt_fusion.4, f32[32,128]{1,0:T(8,128)S(1)} %broadcast_multiply_fusion.4, bf16[192,768]{1,0:T(8,128)(2,1)S(1)} %copy-done), kind=kOutput, calls=%fused_computation.56 | convolution fusion | flops 1227620352 | bytes 8192768 | tf_op jit(solution)/shard_map/dot_general | solution.py:30
  23.2 5.2 %collective-permute-start.2 = (bf16[34,192]{1,0:T(8,128)(2,1)S(1)}, bf16[34,192]{1,0:T(8,128)(2,1)S(1)}, u32[]{:S(2)}, u32[]{:S(2)}) collective-permute-start(bf16[34,192]{1,0:T(8,128)(2,1)S(1)} %pad_maximum_fusion.4), channel_id=1, source_target_pairs={{0,1},{1,2},{2,3},{3,4},{4,5},{5,6},{6,7},{8,9},{9,10},{10,11},{11... | collective-permute-start | bytes 39176 | tf_op jit(solution)/shard_map/ppermute | solution.py:110
  38.0 10.1 %maximum_maximum_fusion = (bf16[34,129,768]{2,1,0:T(8,128)(2,1)S(1)}, bf16[34,129,768]{2,1,0:T(8,128)(2,1)S(1)}) fusion(bf16[1,128,768]{2,1,0:T(8,128)(2,1)S(1)} %get-tuple-element.99, bf16[32,128,768]{2,1,0:T(8,128)(2,1)} %multiply_convert_fusion.17, bf16[1,128,768]{2,1,0:T(8,128)(2,1)S(1)} %get-tuple-element.98, bf16[34,1,768]{2,1,0:T(2,128)(2,1)S(1)} %copy.57, ...), kind=kLoop, calls=%fused_computation.57 | loop fusion | flops 53895168 | bytes 20262912 | tf_op jit(solution)/shard_map/concatenate | solution.py:121
  48.1 21.9 %fusion.105 = bf16[32,128,192]{1,2,0:T(8,128)(2,1)S(1)} fusion(bf16[32,128,192]{1,2,0:T(8,128)(2,1)S(1)} %copy-done.3, bf16[32,128,768]{2,1,0:T(8,128)(2,1)} %multiply_convert_fusion.17, bf16[34,129,768]{2,1,0:T(8,128)(2,1)S(1)} %get-tuple-element.91, bf16[1,128,768]{2,1,0:T(8,128)(2,1)S(1)} %get-tuple-element.99, ...), kind=kOutput, calls=%fused_computation.108 | convolution fusion | flops 1326710784 | bytes 47910912 | tf_op jit(solution)/shard_map/dot_general | solution.py:30
  70.0 2.6 copy.59
  76.6 3.0 %convolution_convert_fusion = bf16[64,64,6,32]{1,3,2,0:T(8,128)(2,1)} fusion(bf16[192,3,6,32]{0,3,2,1:T(8,128)(2,1)S(1)} %bitcast.214, bf16[64,64,192]{2,1,0:T(8,128)(2,1)S(1)} %bitcast.195, f32[192]{0:T(256)S(1)} %copy-done.16, f32[64,64]{1,0:T(8,128)S(1)} %add_rsqrt_fusion.1, f32[64,64]{1,0:T(8,128)S(1)} %broadcast_multiply_fusion.1), kind=kOutput, calls=%fused_computation.111 | convolution fusion | flops 306708480 | bytes 3834880 | tf_op jit(solution)/shard_map/gtc,chd->ghtd/dot_general | solution.py:40
  79.6 3.0 %convolution_convert_fusion.1 = bf16[64,64,6,32]{1,3,2,0:T(8,128)(2,1)} fusion(bf16[192,3,6,32]{0,3,2,1:T(8,128)(2,1)S(1)} %bitcast.215, bf16[64,64,192]{2,1,0:T(8,128)(2,1)S(1)} %bitcast.196, f32[192]{0:T(256)S(1)} %copy-done.16, f32[64,64]{1,0:T(8,128)S(1)} %add_rsqrt_fusion.1, f32[64,64]{1,0:T(8,128)S(1)} %broadcast_multiply_fusion.1), kind=kOutput, calls=%fused_computation.112 | convolution fusion | flops 306708480 | bytes 3834880 | tf_op jit(solution)/shard_map/gtc,chd->ghtd/dot_general | solution.py:40
  82.5 3.1 %convolution_convert_fusion.2 = bf16[64,64,6,32]{1,3,2,0:T(8,128)(2,1)} fusion(bf16[192,3,6,32]{0,3,2,1:T(8,128)(2,1)S(1)} %bitcast.216, bf16[64,64,192]{2,1,0:T(8,128)(2,1)S(1)} %bitcast.197, f32[192]{0:T(256)S(1)} %copy-done.16, f32[64,64]{1,0:T(8,128)S(1)} %add_rsqrt_fusion.1, f32[64,64]{1,0:T(8,128)S(1)} %broadcast_multiply_fusion.1), kind=kOutput, calls=%fused_computation.113 | convolution fusion | flops 306708480 | bytes 3834880 | tf_op jit(solution)/shard_map/gtc,chd->ghtd/dot_general | solution.py:40
  85.6 28.1 %while.20 = (s32[]{:T(128)}, bf16[2,32,64,6,32]{2,4,3,1,0:T(8,128)(2,1)}, bf16[2,32,6,64,32]{3,4,2,1,0:T(8,128)(2,1)}, bf16[2,32,6,64,32]{3,4,2,1,0:T(8,128)(2,1...) while((s32[]{:T(128)}, bf16[2,32,64,6,32]{2,4,3,1,0:T(8,128)(2,1)}, ...), condition=%wide.region_9.10_spmd, body=%wide.region_6.9_spmd.sunk | while | flops 108159104 | bytes 37947488 | solution.py:60
  86.1 2.9 %fusion.203 = f32[32,6,64,64]{2,3,1,0:T(8,128)S(1)} fusion(bf16[2,32,6,64,32]{3,4,2,1,0:T(8,128)(2,1)} %get-tuple-element.186, s32[]{:T(128)} %get-tuple-element.176, bf16[2,32,6,64,32]{3,4,2,1,0:T(8,128)(2,1)} %get-tuple-element.185), kind=kOutput, calls=%fused_computation.10.clone.1 | convolution fusion | flops 50331648 | bytes 6292480 | tf_op jit(solution)/shard_map/while/body/eval_jaxpr/ghtd,ghsd->ghts/dot_general | solution.py:48
  89.1 1.9 fusion.204
  91.8 8.1 %bitcast_dynamic-update-slice_fusion.2 = bf16[2,32,64,6,32]{2,4,3,1,0:T(8,128)(2,1)} fusion(bf16[2,32,64,6,32]{2,4,3,1,0:T(8,128)(2,1)} %get-tuple-element.177, s32[]{:T(128)} %get-tuple-element.176, f32[32,6,64]{2,1,0:T(8,128)S(1)} %broadcast_divide_fusion.4, bf16[2,32,6,64,32]{3,4,2,1,0:T(8,128)(2,1)} %get-tuple-element.184, ...), kind=kOutput, calls=%fused_computation.9.clone.1 | convolution fusion | flops 54669376 | bytes 15778816 | tf_op jit(solution)/shard_map/while/body/eval_jaxpr/ghts,ghsd->gthd/dot_general | solution.py:55
  99.9 2.9 fusion.203
  105.5 8.2 %bitcast_dynamic-update-slice_fusion.2 = bf16[2,32,64,6,32]{2,4,3,1,0:T(8,128)(2,1)} fusion(bf16[2,32,64,6,32]{2,4,3,1,0:T(8,128)(2,1)} %get-tuple-element.177, s32[]{:T(128)} %get-tuple-element.176, f32[32,6,64]{2,1,0:T(8,128)S(1)} %broadcast_divide_fusion.4, bf16[2,32,6,64,32]{3,4,2,1,0:T(8,128)(2,1)} %get-tuple-element.184, ...), kind=kOutput, calls=%fused_computation.9.clone.1 | convolution fusion | flops 54669376 | bytes 15778816 | tf_op jit(solution)/shard_map/while/body/eval_jaxpr/ghts,ghsd->gthd/dot_general | solution.py:55
  113.7 3.6 %convert_reduce_fusion = (f32[64,64]{1,0:T(8,128)S(1)}, bf16[64,64,192]{2,1,0:T(8,128)(2,1)S(1)}) fusion(bf16[64,64,192]{1,2,0:T(8,128)(2,1)} %bitcast.209, bf16[192,192]{1,0:T(8,128)(2,1)S(1)} %copy-done.8, bf16[64,64,192]{2,1,0:T(8,128)(2,1)S(1)} %bitcast.198), kind=kOutput, calls=%fused_computation.63 | convolution fusion | flops 305917952 | bytes 4808704 | tf_op jit(solution)/shard_map/dot_general | solution.py:30
  120.0 6.3 %fusion.85 = bf16[64,64,192]{2,1,0:T(8,128)(2,1)S(1)} fusion(bf16[64,64,192]{2,1,0:T(8,128)(2,1)} %copy-done.5, f32[192]{0:T(256)S(1)} %copy-done.17, f32[64,64]{1,0:T(8,128)S(1)} %add_rsqrt_fusion, f32[64,64]{1,0:T(8,128)S(1)} %broadcast_multiply_fusion, bf16[768,192]{0,1:T(8,128)(2,1)S(1)} %copy-done.11, bf16[192,768]{1,0:T(8,128)(2,1)S(1)} %copy-done.12), kind=kOutput, calls=%fused_computation.90 | convolution fusion | flops 2437939200 | bytes 3769088 | tf_op jit(solution)/shard_map/dot_general | solution.py:30
  126.5 3.3 %copy.64 = bf16[16,8,2,8,1,2,192]{6,5,3,2,1,0,4:T(2,128)(2,1)S(1)} copy(bf16[16,8,2,8,1,2,192]{6,3,1,5,2,0,4:T(8,128)(2,1)S(1)} %bitcast.206) | data formatting | bytes 3145728 | tf_op jit(solution)/shard_map/transpose | solution.py:155
  129.8 3.0 %reshape.179 = bf16[128,48,128]{2,1,0:T(8,128)(2,1)} reshape(bf16[16,8,2,8,1,2,192]{6,5,3,2,1,0,4:T(2,128)(2,1)S(1)} %copy.64) | data formatting | bytes 3145728 | tf_op jit(solution)/shard_map/reshape | solution.py:157
  132.9 10.5 %all-to-all-start = ((bf16[128,48,128]{2,1,0:T(8,128)(2,1)}), bf16[128,48,128]{2,1,0:T(8,128)(2,1)S(1)}, u32[]{:S(2)}, u32[]{:S(2)}) async-start(bf16[128,48,128]{2,1,0:T(8,128)(2,1)} %reshape.179), calls=%async_computation | async-start | bytes 3145728 | tf_op jit(solution)/shard_map/all_to_all | solution.py:158
  143.5 24.8 %all-to-all-done = bf16[128,48,128]{2,1,0:T(8,128)(2,1)S(1)} async-done(((bf16[128,48,128]{2,1,0:T(8,128)(2,1)}), bf16[128,48,128]{2,1,0:T(8,128)(2,1)S(1)}, u32[]{:S(2)}, u32[]{:S(2)}) %all-to-all-start) | async-done | bytes 1572896 | tf_op jit(solution)/shard_map/all_to_all | solution.py:158
  169.5 3.0 %copy.66 = bf16[2,8,128,2,192]{4,1,0,3,2:T(8,128)(2,1)} copy(bf16[2,8,128,2,192]{2,4,3,1,0:T(8,128)(2,1)S(1)} %bitcast.207) | data formatting | bytes 3145728 | tf_op jit(solution)/shard_map/transpose | solution.py:161
  172.5 3.5 %copy.67 = bf16[16,256,192]{1,2,0:T(8,128)(2,1)S(1)} copy(bf16[16,256,192]{2,0,1:T(8,128)(2,1)} %bitcast.201) | data formatting | bytes 3145728 | tf_op jit(solution)/shard_map/optimization_barrier | solution.py:164
  182.3 51.9 %while.21 = (s32[]{:T(128)}, bf16[8,2,256,6,32]{2,4,3,1,0:T(8,128)(2,1)}, bf16[8,2,6,256,32]{3,4,2,1,0:T(8,128)(2,1)}, bf16[8,2,6,256,32]{3,4,2,1,0:T(8,128)(2,1...) while((s32[]{:T(128)}, bf16[8,2,256,6,32]{2,4,3,1,0:T(8,128)(2,1)}, ...), condition=%wide.region_17.18_spmd, body=%wide.region_14.17_spmd.sunk | while | flops 157391360 | bytes 10673221 | solution.py:60
  184.0 2.2 fusion.211
  186.2 2.6 fusion.213
  190.5 2.2 fusion.211
  192.7 2.6 fusion.213
  196.9 2.2 fusion.211
  199.1 2.6 fusion.213
  203.4 2.2 fusion.211
  205.6 2.6 fusion.213
  209.8 2.2 fusion.211
  212.0 2.6 fusion.213
  216.3 2.2 fusion.211
  218.5 2.6 fusion.213
  222.7 2.2 fusion.211
  224.9 2.6 fusion.213
  229.2 2.2 fusion.211
  231.4 2.6 fusion.213
  234.3 2.6 convert_reduce_fusion.2
  237.4 6.0 %fusion.107 = bf16[16,256,192]{1,2,0:T(8,128)(2,1)} fusion(bf16[16,256,192]{1,2,0:T(8,128)(2,1)S(1)} %get-tuple-element.107, f32[192]{0:T(256)S(1)} %copy-done.19, f32[16,256]{1,0:T(8,128)S(1)} %add_rsqrt_fusion.2, f32[16,256]{1,0:T(8,128)S(1)} %broadcast_multiply_fusion.2, bf16[768,192]{0,1:T(8,128)(2,1)S(1)} %copy-done.13, ...), kind=kOutput, calls=%fused_computation.110 | convolution fusion | flops 2437939200 | bytes 3769088 | tf_op jit(solution)/shard_map/dot_general | solution.py:30
  243.4 3.2 %copy.70 = bf16[16,256,192]{2,0,1:T(8,128)(2,1)S(1)} copy(bf16[16,256,192]{1,2,0:T(8,128)(2,1)} %fusion.107) | data formatting | bytes 3145728 | tf_op jit(solution)/shard_map/convert_element_type | solution.py:68
  246.7 2.9 %copy.71 = bf16[128,2,8,2,192]{0,4,3,2,1:T(8,128)(2,1)} copy(bf16[128,2,8,2,192]{4,2,1,3,0:T(8,128)(2,1)S(1)} %bitcast.202) | data formatting | bytes 3145728 | tf_op jit(solution)/shard_map/transpose | solution.py:169
  249.6 2.0 copy.72
  251.6 29.0 %all_to_all.10 = bf16[128,48,128]{2,1,0:T(8,128)(2,1)} all-to-all(bf16[128,48,128]{2,1,0:T(8,128)(2,1)S(1)} %copy.72), channel_id=1, replica_groups=mesh['rows'=16,'cols'=8] {'rows','cols'}, dimensions={0} | all-to-all | bytes 3145728 | tf_op jit(solution)/shard_map/all_to_all | solution.py:170
  280.6 5.1 %reshape.188 = bf16[16,8,2,8,1,2,192]{6,5,3,2,1,0,4:T(2,128)(2,1)S(1)} reshape(bf16[128,48,128]{2,1,0:T(8,128)(2,1)} %all_to_all.10) | data formatting | bytes 3145728 | tf_op jit(solution)/shard_map/reshape | solution.py:172
  287.5 3.9 %copy.74 = bf16[32,128,192]{1,2,0:T(8,128)(2,1)} copy(bf16[32,128,192]{2,1,0:T(8,128)(2,1)} %bitcast.205) | data formatting | bytes 3145728 | tf_op jit(solution)/shard_map/reshape | solution.py:176
  (116 shorter events, 56.0 us)
Async XLA Ops:
  0.0 12.9 %copy-start = (bf16[192,768]{1,0:T(8,128)(2,1)S(1)}, bf16[192,768]{1,0:T(8,128)(2,1)}, u32[]{:S(2)}) copy-start(bf16[192,768]{1,0:T(8,128)(2,1)} %param.23) | copy-start | bytes 884740
  0.0 12.9 %copy-start.3 = (bf16[32,128,192]{1,2,0:T(8,128)(2,1)S(1)}, bf16[32,128,192]{1,2,0:T(8,128)(2,1)}, u32[]{:S(2)}) copy-start(bf16[32,128,192]{1,2,0:T(8,128)(2,1)} %param.21) | copy-start | bytes 4718596
  0.0 12.9 %copy-start.15 = (f32[192]{0:T(256)S(1)}, f32[192]{0:T(256)}, u32[]{:S(2)}) copy-start(f32[192]{0:T(256)} %param.22) | copy-start | bytes 2308
  1.7 20.7 %collective-permute-start = (bf16[128,192]{1,0:T(8,128)(2,1)}, bf16[128,192]{1,0:T(8,128)(2,1)S(1)}, u32[]{:S(2)}, u32[]{:S(2)}) collective-permute-start(bf16[128,192]{1,0:T(8,128)(2,1)} %bitcast.10), channel_id=1, source_target_pairs={{0,8},{8,16},{16,24},{24,32},{32,40},{40,48},{48,56},{56,64},{64,7... | collective-permute-start | bytes 147464 | tf_op jit(solution)/shard_map/ppermute | solution.py:104
  7.4 15.1 %collective-permute-start.1 = (bf16[128,192]{1,0:T(8,128)(2,1)}, bf16[128,192]{1,0:T(8,128)(2,1)}, u32[]{:S(2)}, u32[]{:S(2)}) collective-permute-start(bf16[128,192]{1,0:T(8,128)(2,1)} %bitcast.11), channel_id=1, source_target_pairs={{8,0},{16,8},{24,16},{32,24},{40,32},{48,40},{56,48},{64,56},{72,6... | collective-permute-start | bytes 147464 | tf_op jit(solution)/shard_map/ppermute | solution.py:105
  23.2 9.6 %collective-permute-start.2 = (bf16[34,192]{1,0:T(8,128)(2,1)S(1)}, bf16[34,192]{1,0:T(8,128)(2,1)S(1)}, u32[]{:S(2)}, u32[]{:S(2)}) collective-permute-start(bf16[34,192]{1,0:T(8,128)(2,1)S(1)} %pad_maximum_fusion.4), channel_id=1, source_target_pairs={{0,1},{1,2},{2,3},{3,4},{4,5},{5,6},{6,7},{8,9},{9,10},{10,11},{11... | collective-permute-start | bytes 39176 | tf_op jit(solution)/shard_map/ppermute | solution.py:110
  28.4 6.0 %collective-permute-start.3 = (bf16[34,192]{1,0:T(8,128)(2,1)S(1)}, bf16[34,192]{1,0:T(8,128)(2,1)S(1)}, u32[]{:S(2)}, u32[]{:S(2)}) collective-permute-start(bf16[34,192]{1,0:T(8,128)(2,1)S(1)} %pad_maximum_fusion.5), channel_id=1, source_target_pairs={{1,0},{2,1},{3,2},{4,3},{5,4},{6,5},{7,6},{9,8},{10,9},{11,10},{12... | collective-permute-start | bytes 39176 | tf_op jit(solution)/shard_map/ppermute | solution.py:111
  38.0 10.1 %copy-start.10 = (bf16[768,192]{0,1:T(8,128)(2,1)S(1)}, bf16[768,192]{0,1:T(8,128)(2,1)}, u32[]{:S(2)}) copy-start(bf16[768,192]{0,1:T(8,128)(2,1)} %param.25) | copy-start | bytes 884740
  74.5 2.0 copy-start.6
  74.5 2.0 copy-start.16
  85.6 28.1 %copy-start.8 = (bf16[192,192]{1,0:T(8,128)(2,1)S(1)}, bf16[192,192]{1,0:T(8,128)(2,1)}, u32[]{:S(2)}) copy-start(bf16[192,192]{1,0:T(8,128)(2,1)} %param.28) | copy-start | bytes 221188
  89.1 2.7 copy-start.2
  102.8 2.7 copy-start.2
  113.7 6.3 %copy-start.11 = (bf16[768,192]{0,1:T(8,128)(2,1)S(1)}, bf16[768,192]{0,1:T(8,128)(2,1)}, u32[]{:S(2)}) copy-start(bf16[768,192]{0,1:T(8,128)(2,1)} %param.31) | copy-start | bytes 884740
  113.7 6.3 %copy-start.12 = (bf16[192,768]{1,0:T(8,128)(2,1)S(1)}, bf16[192,768]{1,0:T(8,128)(2,1)}, u32[]{:S(2)}) copy-start(bf16[192,768]{1,0:T(8,128)(2,1)} %param.30) | copy-start | bytes 884740
  113.7 6.3 %copy-start.17 = (f32[192]{0:T(256)S(1)}, f32[192]{0:T(256)}, u32[]{:S(2)}) copy-start(f32[192]{0:T(256)} %param.29) | copy-start | bytes 2308
  117.3 1.4 copy-start.5
  129.8 13.5 %copy-start.7 = (bf16[192,576]{1,0:T(8,128)(2,1)S(1)}, bf16[192,576]{1,0:T(8,128)(2,1)}, u32[]{:S(2)}) copy-start(bf16[192,576]{1,0:T(8,128)(2,1)} %param.33) | copy-start | bytes 663556
  132.9 35.5 %all-to-all-start = ((bf16[128,48,128]{2,1,0:T(8,128)(2,1)}), bf16[128,48,128]{2,1,0:T(8,128)(2,1)S(1)}, u32[]{:S(2)}, u32[]{:S(2)}) async-start(bf16[128,48,128]{2,1,0:T(8,128)(2,1)} %reshape.179), calls=%async_computation | async-start | bytes 3145728 | tf_op jit(solution)/shard_map/all_to_all | solution.py:158
  172.5 4.2 %copy-start.18 = (f32[192]{0:T(256)S(1)}, f32[192]{0:T(256)}, u32[]{:S(2)}) copy-start(f32[192]{0:T(256)} %param.32) | copy-start | bytes 2308
  176.0 6.3 %copy-start.4 = (bf16[16,256,192]{1,2,0:T(8,128)(2,1)}, bf16[16,256,192]{1,2,0:T(8,128)(2,1)S(1)}, u32[]{:S(2)}) copy-start(bf16[16,256,192]{1,2,0:T(8,128)(2,1)S(1)} %copy.67) | copy-start | bytes 4718596
  182.3 51.9 %copy-start.9 = (bf16[192,192]{1,0:T(8,128)(2,1)S(1)}, bf16[192,192]{1,0:T(8,128)(2,1)}, u32[]{:S(2)}) copy-start(bf16[192,192]{1,0:T(8,128)(2,1)} %param.34) | copy-start | bytes 221188
  234.2 3.2 %copy-start.13 = (bf16[768,192]{0,1:T(8,128)(2,1)S(1)}, bf16[768,192]{0,1:T(8,128)(2,1)}, u32[]{:S(2)}) copy-start(bf16[768,192]{0,1:T(8,128)(2,1)} %param.37) | copy-start | bytes 884740
  234.2 3.2 %copy-start.14 = (bf16[192,768]{1,0:T(8,128)(2,1)S(1)}, bf16[192,768]{1,0:T(8,128)(2,1)}, u32[]{:S(2)}) copy-start(bf16[192,768]{1,0:T(8,128)(2,1)} %param.36) | copy-start | bytes 884740
  234.2 3.2 %copy-start.19 = (f32[192]{0:T(256)S(1)}, f32[192]{0:T(256)}, u32[]{:S(2)}) copy-start(f32[192]{0:T(256)} %param.35) | copy-start | bytes 2308
  285.7 5.7 %copy-start.1 = (bf16[192,768]{1,0:T(8,128)(2,1)S(1)}, bf16[192,768]{1,0:T(8,128)(2,1)}, u32[]{:S(2)}) copy-start(bf16[192,768]{1,0:T(8,128)(2,1)} %param.23) | copy-start | bytes 884740

commit v4 on v1

--- a/solution.py
+++ b/solution.py
@@ -34,21 +34,22 @@
 def attend(normed, w_qkv, w_out):
     groups, tokens, channels = normed.shape
     head_size = channels // HEADS
-    qkv_all = project(normed, w_qkv).astype(jnp.bfloat16)
-    heads_split = qkv_all.reshape(groups, tokens, 3, HEADS, head_size)
+    w_split = w_qkv.reshape(channels, 3, HEADS, head_size)
+
+    def heads_of(part):
+        return jnp.einsum(
+            "gtc,chd->ghtd", normed, w_split[:, part], preferred_element_type=jnp.float32
+        ).astype(jnp.bfloat16)
+
+    queries, keys, values = heads_of(0), heads_of(1), heads_of(2)
     scores = jnp.einsum(
-        "gthd,gshd->ghts",
-        heads_split[:, :, 0],
-        heads_split[:, :, 1],
-        preferred_element_type=jnp.float32,
+        "ghtd,ghsd->ghts", queries, keys, preferred_element_type=jnp.float32
     ) * head_size ** (-0.5)
     peak = jnp.max(scores, axis=-1, keepdims=True)
     lifted = jnp.exp(scores - peak)
     total = jnp.sum(lifted, axis=-1, keepdims=True)
     weights = (lifted * (1.0 / total)).astype(jnp.bfloat16)
-    mixed = jnp.einsum(
-        "ghts,gshd->gthd", weights, heads_split[:, :, 2], preferred_element_type=jnp.float32
-    )
+    mixed = jnp.einsum("ghts,ghsd->gthd", weights, values, preferred_element_type=jnp.float32)
     mixed = mixed.astype(jnp.bfloat16).reshape(groups, tokens, channels)
     return project(mixed, w_out)
 
@@ -157,8 +158,8 @@
     grid_attn = (tokens.astype(jnp.float32) + update.astype(jnp.float32)).astype(jnp.bfloat16)
     grid_out = feed_forward(grid_attn, gain_gffn, ffn_in_grid, ffn_out_grid)
     grid_out = grid_out.reshape(part_rows, part_cols, devices, local_rows * local_cols, channels)
-    packed = grid_out.transpose(2, 0, 1, 3, 4).reshape(devices, -1, 128)
-    returned = lax.all_to_all(packed, both, split_axis=0, concat_axis=0, tiled=True)
+    outgoing = grid_out.transpose(2, 0, 1, 3, 4)
+    returned = lax.all_to_all(outgoing, both, split_axis=0, concat_axis=0, tiled=True)
     return (
         returned.reshape(
             rows_count, cols_count, part_rows, part_cols, local_rows, local_cols, channels

time: 275 us -> 255 us (0.927)
  blocking collectives: 65.8 us -> 34.4 us
  waiting for transfers between devices: 0.01 us -> 24.8 us
  local copies, waits for them, and re-layouts: 57.2 us -> 37.3 us
  starting transfers between devices: 14.5 us -> 25.9 us
  matrix products: 94.6 us -> 90.1 us
    all_to_all x2 -> x1, blocking collectives: 65.8 us -> 34.4 us  [shards_body(): lax.all_to_all(outgoing, both, split_axis=0, concat_axis=0, tiled=True)]
    all_to_all x0 -> x1, waiting for transfers between devices: none -> 24.8 us  [shards_body(): lax.all_to_all(packed, both, split_axis=0, concat_axis=0, tiled=True)]
    all_to_all x0 -> x1, starting transfers between devices: none -> 11.4 us  [shards_body(): lax.all_to_all(packed, both, split_axis=0, concat_axis=0, tiled=True)]
    convert_element_type x1 -> x0, local copies, waits for them, and re-layouts: 10.2 us -> none  [attend(): qkv_all = project(normed, w_qkv).astype(jnp.bfloat16)]
    dot_general x9 -> x7, matrix products: 52.7 us -> 47.1 us  [project(): output = jnp.dot(flattened, weight, preferred_element_type=jnp.float32)]
    reshape x1, local copies, waits for them, and re-layouts: 5.14 us -> 0.27 us  [shards_body(): returned.reshape(rows_count, cols_count, part_rows, part_cols, local_rows...]
    transpose x2 -> x0, local copies, waits for them, and re-layouts: 4.69 us -> none  [the longest x1 2.93 us: shards_body(): packed = grid_out.transpose(2, 0, 1, 3, 4).reshape(devices, -1, 128)]
    unnamed x36 -> x42, local copies, waits for them, and re-layouts: 5.63 us -> 8.74 us
  transfers between devices with their start and end apart: 4 -> 5, of which waited for: 0 -> 1; matrix products, arithmetic and copies ran while one was open for 6% -> 7% of each run, Pallas kernels for 0% -> 0%
where the time goes in v4:
time: 255 us; the launch traced here: 251 us
  matrix products  90.1 us (35%)
  other arithmetic  37.6 us (15%)
  local copies, waits for them, and re-layouts  37.3 us (15%)
  blocking collectives  34.4 us (13%)
  starting transfers between devices  25.9 us (10%)
  waiting for transfers between devices  24.8 us (10%)
    dot_general x7, matrix products, project(): output = jnp.dot(flattened, weight, preferred_element_type=jnp.float32)  47.1 us
    all_to_all x1, blocking collectives, shards_body(): lax.all_to_all(outgoing, both, split_axis=0, concat_axis=0, tiled=True)  34.4 us
    all_to_all x1, waiting for transfers between devices, shards_body(): lax.all_to_all(packed, both, split_axis=0, concat_axis=0, tiled=True)  24.8 us
    dot_general x2, matrix products, attend(): jnp.einsum('ghts,ghsd->gthd', weights, values, preferred_element_type=jnp...  18.6 us
    sub x1, other arithmetic, attend(): lifted = jnp.exp(scores - peak)  16.4 us
    sub x1, matrix products, attend(): lifted = jnp.exp(scores - peak)  14.2 us
    all_to_all x1, starting transfers between devices, shards_body(): lax.all_to_all(packed, both, split_axis=0, concat_axis=0, tiled=True)  11.4 us
    concatenate x1, other arithmetic, shards_body(): expanded = jnp.concatenate([left, expanded, right], axis=1)  10.1 us
  transfers between devices with their start and end apart: 5, of which 1 were waited for; matrix products, arithmetic and copies ran while one was open for 7% of the time, Pallas kernels for 0%

profile of v4, /device:TPU:1, one launch (start us, length us, event | category | flops | bytes accessed | tf_op | source)
XLA Modules:
  0.0 251.0 jit_solution(2604800916836820686)
XLA Ops:
  0.0 0.9 fusion.147
  0.9 0.7 copy.78
  1.6 3.3 %collective-permute-start.1 = (bf16[128,192]{1,0:T(8,128)(2,1)}, bf16[128,192]{1,0:T(8,128)(2,1)S(1)}, u32[]{:S(2)}, u32[]{:S(2)}) collective-permute-start(bf16[128,192]{1,0:T(8,128)(2,1)} %bitcast.1), channel_id=1, source_target_pairs={{8,0},{16,8},{24,16},{32,24},{40,32},{48,40},{56,48},{64,56},{72,6... | collective-permute-start | bytes 147464 | tf_op jit(solution)/shard_map/ppermute | solution.py:97
  4.9 0.7 copy.77
  5.6 3.5 %collective-permute-start = (bf16[128,192]{1,0:T(8,128)(2,1)}, bf16[128,192]{1,0:T(8,128)(2,1)}, u32[]{:S(2)}, u32[]{:S(2)}) collective-permute-start(bf16[128,192]{1,0:T(8,128)(2,1)} %bitcast), channel_id=1, source_target_pairs={{0,8},{8,16},{16,24},{24,32},{32,40},{40,48},{48,56},{56,64},{64,7... | collective-permute-start | bytes 147464 | tf_op jit(solution)/shard_map/ppermute | solution.py:96
  9.2 1.7 convert_reduce_fusion.4
  10.9 1.9 fusion.45
  12.8 5.9 %multiply_convert_fusion.6 = bf16[32,128,768]{2,1,0:T(8,128)(2,1)} fusion(bf16[32,128,192]{1,2,0:T(8,128)(2,1)} %param.17, f32[192]{0:T(256)} %param.18, f32[32,128]{1,0:T(8,128)S(1)} %add_rsqrt_fusion.4, f32[32,128]{1,0:T(8,128)S(1)} %broadcast_multiply_fusion.4, bf16[192,768]{1,0:T(8,128)(2,1)S(1)} %copy-done), kind=kOutput, calls=%fused_computation.14 | convolution fusion | flops 1227620352 | bytes 8192768 | tf_op jit(solution)/shard_map/dot_general | solution.py:30
  18.7 1.8 fusion.146
  20.5 1.9 copy.79
  22.4 0.9 copy.80
  23.3 0.7 fusion.148
  24.0 1.3 collective-permute-start.3
  25.4 6.4 %collective-permute-start.2 = (bf16[34,192]{1,0:T(8,128)(2,1)S(1)}, bf16[34,192]{1,0:T(8,128)(2,1)S(1)}, u32[]{:S(2)}, u32[]{:S(2)}) collective-permute-start(bf16[34,192]{1,0:T(8,128)(2,1)S(1)} %pad_maximum_fusion.4), channel_id=1, source_target_pairs={{0,1},{1,2},{2,3},{3,4},{4,5},{5,6},{6,7},{8,9},{9,10},{10,11},{11... | collective-permute-start | bytes 39176 | tf_op jit(solution)/shard_map/ppermute | solution.py:102
  31.7 0.9 convert_reduce_fusion.14
  32.7 1.8 copy.56
  34.5 1.0 convert_reduce_fusion.5
  35.5 1.1 fusion.113
  36.6 1.2 multiply_convert_fusion.21
  38.1 10.1 %maximum_maximum_fusion = (bf16[34,129,768]{2,1,0:T(8,128)(2,1)S(1)}, bf16[34,129,768]{2,1,0:T(8,128)(2,1)S(1)}) fusion(bf16[1,128,768]{2,1,0:T(8,128)(2,1)S(1)} %get-tuple-element.23, bf16[32,128,768]{2,1,0:T(8,128)(2,1)} %multiply_convert_fusion.6, bf16[1,128,768]{2,1,0:T(8,128)(2,1)S(1)} %get-tuple-element.22, bf16[34,1,768]{2,1,0:T(2,128)(2,1)S(1)} %copy.52, ...), kind=kLoop, calls=%fused_computation.17 | loop fusion | flops 53895168 | bytes 20262912 | tf_op jit(solution)/shard_map/concatenate | solution.py:113
  48.2 21.9 %fusion.48 = bf16[32,128,192]{1,2,0:T(8,128)(2,1)S(1)} fusion(bf16[32,128,192]{1,2,0:T(8,128)(2,1)S(1)} %copy-done.2, bf16[32,128,768]{2,1,0:T(8,128)(2,1)} %multiply_convert_fusion.6, bf16[34,129,768]{2,1,0:T(8,128)(2,1)S(1)} %get-tuple-element.15, bf16[1,128,768]{2,1,0:T(8,128)(2,1)S(1)} %get-tuple-element.23, ...), kind=kOutput, calls=%fused_computation.71 | convolution fusion | flops 1326710784 | bytes 47910912 | tf_op jit(solution)/shard_map/dot_general | solution.py:30
  70.1 2.6 %copy.54 = bf16[32,128,192]{2,1,0:T(8,128)(2,1)} copy(bf16[32,128,192]{1,2,0:T(8,128)(2,1)S(1)} %fusion.48) | data formatting | bytes 3145728 | tf_op jit(solution)/shard_map/convert_element_type | solution.py:121
  72.7 1.9 copy.55
  75.3 1.3 fusion.24
  76.6 7.7 %fusion.51 = f32[64,6,64,64]{2,3,1,0:T(8,128)} fusion(bf16[64,64,192]{2,1,0:T(8,128)(2,1)S(1)} %bitcast.161, f32[192]{0:T(256)S(1)} %copy-done.10, f32[64,64]{1,0:T(8,128)S(1)} %add_rsqrt_fusion.1, f32[64,64]{1,0:T(8,128)S(1)} %broadcast_multiply_fusion.1, bf16[192,3,6,32]{0,3,2,1:T(8,128)(2,1)S(1)} %bitcast.174), kind=kOutput, calls=%fused_computation.74 | convolution fusion | flops 714080256 | bytes 10815488 | tf_op jit(solution)/shard_map/ghtd,ghsd->ghts/dot_general | solution.py:45
  84.3 16.4 %fusion.150 = (f32[64,6,64]{2,1,0:T(8,128)S(1)}, f32[64,6,64,64]{2,3,1,0:T(8,128)}) fusion(f32[64,6,64,64]{2,3,1,0:T(8,128)} %fusion.51), kind=kOutput, calls=%fused_computation.179 | output fusion | flops 6291519 | bytes 12681216 | tf_op jit(solution)/shard_map/sub | solution.py:49
  100.8 7.5 %fusion.64 = bf16[64,6,32,64]{3,2,1,0:T(8,128)(2,1)} fusion(f32[64,6,64,64]{2,3,1,0:T(8,128)} %get-tuple-element.29, f32[64,6,64]{2,1,0:T(8,128)S(1)} %broadcast_divide_fusion, bf16[64,64,192]{2,1,0:T(8,128)(2,1)S(1)} %bitcast.162, f32[192]{0:T(256)S(1)} %copy-done.10, f32[64,64]{1,0:T(8,128)S(1)} %add_rsqrt_fusion.1, ...), kind=kOutput, calls=%fused_computation.84 | convolution fusion | flops 411303936 | bytes 10388480 | tf_op jit(solution)/shard_map/ghts,ghsd->gthd/dot_general | solution.py:52
  108.3 3.6 %convert_reduce_fusion = (f32[64,64]{1,0:T(8,128)S(1)}, bf16[64,64,192]{2,1,0:T(8,128)(2,1)S(1)}) fusion(bf16[64,64,192]{1,2,0:T(8,128)(2,1)} %bitcast.164, bf16[192,192]{1,0:T(8,128)(2,1)S(1)} %copy-done.8, bf16[64,64,192]{2,1,0:T(8,128)(2,1)S(1)} %bitcast.163), kind=kOutput, calls=%fused_computation.24 | convolution fusion | flops 305917952 | bytes 4808704 | tf_op jit(solution)/shard_map/dot_general | solution.py:30
  111.9 1.3 copy-done.3
  113.3 1.3 fusion.21
  114.7 6.1 %fusion.28 = bf16[64,64,192]{2,1,0:T(8,128)(2,1)S(1)} fusion(bf16[64,64,192]{2,1,0:T(8,128)(2,1)} %copy-done.3, f32[192]{0:T(256)S(1)} %copy-done.16, f32[64,64]{1,0:T(8,128)S(1)} %add_rsqrt_fusion, f32[64,64]{1,0:T(8,128)S(1)} %broadcast_multiply_fusion, bf16[768,192]{0,1:T(8,128)(2,1)S(1)} %copy-done.13, bf16[192,768]{1,0:T(8,128)(2,1)S(1)} %copy-done.14), kind=kOutput, calls=%fused_computation.53 | convolution fusion | flops 2437939200 | bytes 3769088 | tf_op jit(solution)/shard_map/dot_general | solution.py:30
  121.0 3.3 %copy.60 = bf16[16,8,2,8,1,2,192]{6,5,3,2,1,0,4:T(2,128)(2,1)S(1)} copy(bf16[16,8,2,8,1,2,192]{6,3,1,5,2,0,4:T(8,128)(2,1)S(1)} %bitcast.169) | data formatting | bytes 3145728 | tf_op jit(solution)/shard_map/transpose | solution.py:147
  124.3 3.0 %reshape.155 = bf16[128,48,128]{2,1,0:T(8,128)(2,1)} reshape(bf16[16,8,2,8,1,2,192]{6,5,3,2,1,0,4:T(2,128)(2,1)S(1)} %copy.60) | data formatting | bytes 3145728 | tf_op jit(solution)/shard_map/reshape | solution.py:149
  127.3 11.4 %all-to-all-start = ((bf16[128,48,128]{2,1,0:T(8,128)(2,1)}), bf16[128,48,128]{2,1,0:T(8,128)(2,1)S(1)}, u32[]{:S(2)}, u32[]{:S(2)}) async-start(bf16[128,48,128]{2,1,0:T(8,128)(2,1)} %reshape.155), calls=%async_computation | async-start | bytes 3145728 | tf_op jit(solution)/shard_map/all_to_all | solution.py:150
  138.9 24.8 %all-to-all-done = bf16[128,48,128]{2,1,0:T(8,128)(2,1)S(1)} async-done(((bf16[128,48,128]{2,1,0:T(8,128)(2,1)}), bf16[128,48,128]{2,1,0:T(8,128)(2,1)S(1)}, u32[]{:S(2)}, u32[]{:S(2)}) %all-to-all-start) | async-done | bytes 1572896 | tf_op jit(solution)/shard_map/all_to_all | solution.py:150
  163.7 1.1 copy.61
  164.9 3.0 %copy.62 = bf16[2,8,128,2,192]{4,1,0,3,2:T(8,128)(2,1)} copy(bf16[2,8,128,2,192]{2,4,3,1,0:T(8,128)(2,1)S(1)} %bitcast.172) | data formatting | bytes 3145728 | tf_op jit(solution)/shard_map/transpose | solution.py:153
  167.9 3.5 %copy.63 = bf16[16,256,192]{1,2,0:T(8,128)(2,1)S(1)} copy(bf16[16,256,192]{2,0,1:T(8,128)(2,1)} %bitcast.165) | data formatting | bytes 3145728 | tf_op jit(solution)/shard_map/optimization_barrier | solution.py:156
  172.1 0.7 convolution_convert_fusion.2
  172.8 1.9 convolution_convert_fusion.1
  174.7 14.2 %fusion.151 = (f32[16,6,256]{2,1,0:T(8,128)S(1)}, f32[16,6,256,256]{2,3,1,0:T(8,128)}) fusion(bf16[16,256,6,32]{1,3,2,0:T(8,128)(2,1)} %convolution_convert_fusion.1, bf16[16,256,6,32]{1,3,2,0:T(8,128)(2,1)S(1)} %convolution_convert_fusion.2), kind=kOutput, calls=%fused_computation.180 | convolution fusion | flops 421527808 | bytes 28409856 | tf_op jit(solution)/shard_map/sub | solution.py:49
  188.9 11.1 %fusion.80 = bf16[16,6,32,256]{3,2,1,0:T(8,128)(2,1)S(1)} fusion(f32[16,6,256,256]{2,3,1,0:T(8,128)} %get-tuple-element.33, f32[16,6,256]{2,1,0:T(8,128)S(1)} %broadcast_divide_fusion.1, bf16[192,3,6,32]{0,3,2,1:T(8,128)(2,1)} %bitcast.178, bf16[16,256,192]{1,2,0:T(8,128)(2,1)S(1)} %copy.63, f32[192]{0:T(256)S(1)} %copy-done.11, ...), kind=kOutput, calls=%fused_computation.94 | convolution fusion | flops 722731008 | bytes 28541696 | tf_op jit(solution)/shard_map/ghts,ghsd->gthd/dot_general | solution.py:52
  200.0 0.7 convert_reduce_fusion.2
  200.8 1.1 copy-done.4
  202.3 7.7 %fusion.50 = bf16[16,256,192]{1,2,0:T(8,128)(2,1)} fusion(bf16[16,256,192]{1,2,0:T(8,128)(2,1)} %copy-done.4, f32[192]{0:T(256)S(1)} %copy-done.17, f32[16,256]{1,0:T(8,128)S(1)} %add_rsqrt_fusion.2, f32[16,256]{1,0:T(8,128)S(1)} %broadcast_multiply_fusion.2, bf16[768,192]{0,1:T(8,128)(2,1)} %param.33, bf16[192,768]{1,0:T(8,128)(2,1)} %param.32), kind=kOutput, calls=%fused_computation.73 | convolution fusion | flops 2437939200 | bytes 3769088 | tf_op jit(solution)/shard_map/dot_general | solution.py:30
  210.0 3.2 %copy.67 = bf16[16,256,192]{2,0,1:T(8,128)(2,1)S(1)} copy(bf16[16,256,192]{1,2,0:T(8,128)(2,1)} %fusion.50) | data formatting | bytes 3145728 | tf_op jit(solution)/shard_map/convert_element_type | solution.py:60
  213.3 34.4 %all_to_all.10 = bf16[128,2,8,2,192]{4,2,1,3,0:T(8,128)(2,1)S(1)} all-to-all(bf16[128,2,8,2,192]{4,2,1,3,0:T(8,128)(2,1)S(1)} %bitcast.167), channel_id=1, replica_groups=mesh['rows'=16,'cols'=8] {'rows','cols'}, dimensions={0} | all-to-all | bytes 3145728 | tf_op jit(solution)/shard_map/all_to_all | solution.py:162
  247.9 2.7 %copy.69 = bf16[32,128,192]{1,2,0:T(8,128)(2,1)} copy(bf16[32,128,192]{2,1,0:T(8,128)(2,1)S(1)} %bitcast.168) | data formatting | bytes 3145728 | tf_op jit(solution)/shard_map/reshape | solution.py:168
  (66 shorter events, 2.9 us)
Async XLA Ops:
  0.0 12.8 %copy-start = (bf16[192,768]{1,0:T(8,128)(2,1)S(1)}, bf16[192,768]{1,0:T(8,128)(2,1)}, u32[]{:S(2)}) copy-start(bf16[192,768]{1,0:T(8,128)(2,1)} %param.19) | copy-start | bytes 884740
  1.6 21.7 %collective-permute-start.1 = (bf16[128,192]{1,0:T(8,128)(2,1)}, bf16[128,192]{1,0:T(8,128)(2,1)S(1)}, u32[]{:S(2)}, u32[]{:S(2)}) collective-permute-start(bf16[128,192]{1,0:T(8,128)(2,1)} %bitcast.1), channel_id=1, source_target_pairs={{8,0},{16,8},{24,16},{32,24},{40,32},{48,40},{56,48},{64,56},{72,6... | collective-permute-start | bytes 147464 | tf_op jit(solution)/shard_map/ppermute | solution.py:97
  5.6 17.7 %collective-permute-start = (bf16[128,192]{1,0:T(8,128)(2,1)}, bf16[128,192]{1,0:T(8,128)(2,1)}, u32[]{:S(2)}, u32[]{:S(2)}) collective-permute-start(bf16[128,192]{1,0:T(8,128)(2,1)} %bitcast), channel_id=1, source_target_pairs={{0,8},{8,16},{16,24},{24,32},{32,40},{40,48},{48,56},{56,64},{64,7... | collective-permute-start | bytes 147464 | tf_op jit(solution)/shard_map/ppermute | solution.py:96
  12.8 5.9 %copy-start.2 = (bf16[32,128,192]{1,2,0:T(8,128)(2,1)S(1)}, bf16[32,128,192]{1,2,0:T(8,128)(2,1)}, u32[]{:S(2)}) copy-start(bf16[32,128,192]{1,2,0:T(8,128)(2,1)} %param.17) | copy-start | bytes 4718596
  18.7 17.8 %copy-start.15 = (f32[192]{0:T(256)S(1)}, f32[192]{0:T(256)}, u32[]{:S(2)}) copy-start(f32[192]{0:T(256)} %param.18) | copy-start | bytes 2308
  24.0 10.4 %collective-permute-start.3 = (bf16[34,192]{1,0:T(8,128)(2,1)S(1)}, bf16[34,192]{1,0:T(8,128)(2,1)S(1)}, u32[]{:S(2)}, u32[]{:S(2)}) collective-permute-start(bf16[34,192]{1,0:T(8,128)(2,1)S(1)} %pad_maximum_fusion.5), channel_id=1, source_target_pairs={{1,0},{2,1},{3,2},{4,3},{5,4},{6,5},{7,6},{9,8},{10,9},{11,10},{12... | collective-permute-start | bytes 39176 | tf_op jit(solution)/shard_map/ppermute | solution.py:103
  25.4 9.1 %collective-permute-start.2 = (bf16[34,192]{1,0:T(8,128)(2,1)S(1)}, bf16[34,192]{1,0:T(8,128)(2,1)S(1)}, u32[]{:S(2)}, u32[]{:S(2)}) collective-permute-start(bf16[34,192]{1,0:T(8,128)(2,1)S(1)} %pad_maximum_fusion.4), channel_id=1, source_target_pairs={{0,1},{1,2},{2,3},{3,4},{4,5},{5,6},{6,7},{8,9},{9,10},{10,11},{11... | collective-permute-start | bytes 39176 | tf_op jit(solution)/shard_map/ppermute | solution.py:102
  38.1 10.1 %copy-start.12 = (bf16[768,192]{0,1:T(8,128)(2,1)S(1)}, bf16[768,192]{0,1:T(8,128)(2,1)}, u32[]{:S(2)}) copy-start(bf16[768,192]{0,1:T(8,128)(2,1)} %param.21) | copy-start | bytes 884740
  72.7 3.9 %copy-start.5 = (bf16[192,576]{0,1:T(8,128)(2,1)S(1)}, bf16[192,576]{0,1:T(8,128)(2,1)}, u32[]{:S(2)}) copy-start(bf16[192,576]{0,1:T(8,128)(2,1)} %copy.56) | copy-start | bytes 663556
  72.7 3.9 %copy-start.10 = (f32[192]{0:T(256)S(1)}, f32[192]{0:T(256)}, u32[]{:S(2)}) copy-start(f32[192]{0:T(256)} %param.22) | copy-start | bytes 2308
  100.8 7.5 %copy-start.8 = (bf16[192,192]{1,0:T(8,128)(2,1)S(1)}, bf16[192,192]{1,0:T(8,128)(2,1)}, u32[]{:S(2)}) copy-start(bf16[192,192]{1,0:T(8,128)(2,1)} %param.24) | copy-start | bytes 221188
  108.3 6.3 %copy-start.13 = (bf16[768,192]{0,1:T(8,128)(2,1)S(1)}, bf16[768,192]{0,1:T(8,128)(2,1)}, u32[]{:S(2)}) copy-start(bf16[768,192]{0,1:T(8,128)(2,1)} %param.27) | copy-start | bytes 884740
  108.3 6.3 %copy-start.14 = (bf16[192,768]{1,0:T(8,128)(2,1)S(1)}, bf16[192,768]{1,0:T(8,128)(2,1)}, u32[]{:S(2)}) copy-start(bf16[192,768]{1,0:T(8,128)(2,1)} %param.26) | copy-start | bytes 884740
  108.3 6.3 %copy-start.16 = (f32[192]{0:T(256)S(1)}, f32[192]{0:T(256)}, u32[]{:S(2)}) copy-start(f32[192]{0:T(256)} %param.25) | copy-start | bytes 2308
  111.9 1.4 copy-start.3
  124.3 14.5 %copy-start.7 = (bf16[192,576]{1,0:T(8,128)(2,1)S(1)}, bf16[192,576]{1,0:T(8,128)(2,1)}, u32[]{:S(2)}) copy-start(bf16[192,576]{1,0:T(8,128)(2,1)} %param.29) | copy-start | bytes 663556
  127.3 36.4 %all-to-all-start = ((bf16[128,48,128]{2,1,0:T(8,128)(2,1)}), bf16[128,48,128]{2,1,0:T(8,128)(2,1)S(1)}, u32[]{:S(2)}, u32[]{:S(2)}) async-start(bf16[128,48,128]{2,1,0:T(8,128)(2,1)} %reshape.155), calls=%async_computation | async-start | bytes 3145728 | tf_op jit(solution)/shard_map/all_to_all | solution.py:150
  138.9 33.9 %copy-start.6 = (bf16[192,576]{0,1:T(8,128)(2,1)}, bf16[192,576]{0,1:T(8,128)(2,1)S(1)}, u32[]{:S(2)}) copy-start(bf16[192,576]{0,1:T(8,128)(2,1)S(1)} %copy.64) | copy-start | bytes 663556
  167.9 4.2 %copy-start.11 = (f32[192]{0:T(256)S(1)}, f32[192]{0:T(256)}, u32[]{:S(2)}) copy-start(f32[192]{0:T(256)} %param.28) | copy-start | bytes 2308
  188.9 11.1 %copy-start.9 = (bf16[192,192]{1,0:T(8,128)(2,1)S(1)}, bf16[192,192]{1,0:T(8,128)(2,1)}, u32[]{:S(2)}) copy-start(bf16[192,192]{1,0:T(8,128)(2,1)} %param.30) | copy-start | bytes 221188
  200.0 2.4 copy-start.17
  200.7 1.1 copy-start.4
  213.2 37.5 %copy-start.1 = (bf16[192,768]{1,0:T(8,128)(2,1)S(1)}, bf16[192,768]{1,0:T(8,128)(2,1)}, u32[]{:S(2)}) copy-start(bf16[192,768]{1,0:T(8,128)(2,1)} %param.19) | copy-start | bytes 884740
